TPU v7x, 32 devices: a whole 2x2x4 slice. The times are simulated.
32 devices in a mesh: dp: 8 (over z, x), tensor: 4 (over y, core).
Axes of the slice: x: 2, y: 2, z: 4, core: 2. Of those that a mesh axis runs over, the one named last changes fastest.
Arguments:
- tokens_in: bfloat16 [16384, 1536], P('dp'), may hold values from -6 to 6
- segments: int32 [16384], P('dp'), may hold values from 0 to 63, never falling along the last dimension, each value on 1 to 1024 neighbouring positions
- pre_gain: float32 [1536], replicated, may hold values from 0.5 to 1.5
- gate_proj: bfloat16 [1536, 3072], P(None, 'tensor'), may hold values from -0.15625 to 0.15625
- value_proj: bfloat16 [1536, 3072], P(None, 'tensor'), may hold values from -0.15625 to 0.15625
- state_proj: bfloat16 [1536, 256], replicated, may hold values from -0.15625 to 0.15625
- step_proj: bfloat16 [1536, 48], P(None, 'tensor'), may hold values from -0.15625 to 0.15625
- conv_value: float32 [4, 3072], P(None, 'tensor'), may hold values from -3 to 3
- conv_value_bias: float32 [3072], P('tensor'), may hold values from -0.5 to 0.5
- conv_state: float32 [4, 256], replicated, may hold values from -3 to 3
- conv_state_bias: float32 [256], replicated, may hold values from -0.5 to 0.5
- step_bias: float32 [48], P('tensor'), may hold values from -6.9 to -2.25
- decay_log: float32 [48], P('tensor'), may hold values from 0 to 2.77
- skip_gain: float32 [48], P('tensor'), may hold values from 0.5 to 1.5
- norm_gain: float32 [3072], P('tensor'), may hold values from 0.5 to 1.5
- out_proj: bfloat16 [3072, 1536], P('tensor'), may hold values from -0.109375 to 0.109375
- grad_out: bfloat16 [16384, 1536], P('dp'), may hold values from -6 to 6
Outputs:
- block_out: bfloat16 [16384, 1536], P('dp')
- grad_in: bfloat16 [16384, 1536], P('dp')
- grad_pre_gain: float32 [1536], replicated
- grad_gate_proj: float32 [1536, 3072], P(None, 'tensor')
- grad_value_proj: float32 [1536, 3072], P(None, 'tensor')
- grad_state_proj: float32 [1536, 256], replicated
- grad_step_proj: float32 [1536, 48], P(None, 'tensor')
- grad_conv_value: float32 [4, 3072], P(None, 'tensor')
- grad_conv_value_bias: float32 [3072], P('tensor')
- grad_conv_state: float32 [4, 256], replicated
- grad_conv_state_bias: float32 [256], replicated
- grad_step_bias: float32 [48], P('tensor')
- grad_decay_log: float32 [48], P('tensor')
- grad_skip_gain: float32 [48], P('tensor')
- grad_norm_gain: float32 [3072], P('tensor')
- grad_out_proj: float32 [3072, 1536], P('tensor')
Inputs may be any that keep to these rules, and one draw needn't show every extreme that they name: `segments`: segment numbers never fall along the tokens.
All inputs are finite; a program needn't handle non-finite values.
Results may differ from a plain program's by a relative error of at most 0.018.
Values may be sent and summed in bfloat16 or wider, within the bound.
No kernel may reach another device: no remote copies, remote signals or barrier semaphores. Data moves between devices by JAX's collectives and lax.ppermute only.
A program may use at most 256 MiB of HBM per device.

v0:
```python
import math

import jax
import jax.numpy as jnp
import numpy as np
from jax import lax
from jax.experimental import pallas as pl
from jax.experimental.pallas import tpu as pltpu
from jax.sharding import PartitionSpec as P


N = 128
K = 4
SEQ_LEN = 1024
T = 128
LANES = 128
HALF = 64
NEG = -1e30
eps_value = 1e-05
f32 = jnp.float32
bf16 = jnp.bfloat16


def dot(a, b):
    return jnp.dot(a, b, preferred_element_type=f32)


def dot_nt(a, b):
    return lax.dot_general(a, b, (((1,), (1,)), ((), ())), preferred_element_type=f32)


def dot_tn(a, b):
    return lax.dot_general(a, b, (((0,), (0,)), ((), ())), preferred_element_type=f32)


def sigmoid(v):
    return 0.5 * jnp.tanh(0.5 * v) + 0.5


def two_terms(v):
    high = v.astype(bf16)
    return high, (v - high.astype(f32)).astype(bf16)


def paired(v):
    high, low = two_terms(v)
    lane = lax.broadcasted_iota(jnp.int32, v.shape, 1)
    return jnp.where(lane < HALF, high, low)


def sum_rows(v):
    total = v[0:8]
    for row in range(8, v.shape[0], 8):
        total = total + v[row : row + 8]
    return total


def head_rows(heads_ref, lane_ref):
    count = heads_ref.shape[1]
    lane_ref[...] = jnp.zeros_like(lane_ref)
    lane_ref[0:2, 0:count] = heads_ref[...]
    lane_ref[0:2, HALF : HALF + count] = heads_ref[...]
    return lane_ref[0:1, :], -jnp.exp(lane_ref[1:2, :])


def head_terms(z_ref, bias, rate, aux, tri_ref, e_ref, ex_ref):
    z = z_ref[...] + bias
    tail = jnp.exp(-jnp.abs(z))
    step = jnp.maximum(z, 0.0) + jnp.log1p(tail)
    high, low = two_terms(step * rate)
    cum = dot(tri_ref[...], high) + dot(tri_ref[...], low)
    end = cum[T - 1 : T]
    dst = jnp.exp(cum) * aux[:, 3:4]
    dend = jnp.exp(end - cum) * aux[:, 4:5]
    total = jnp.exp(jnp.broadcast_to(end, (8, LANES))) * aux[T - 1 : T, 3:4]
    stacked = jnp.concatenate([paired(step), paired(dend), paired(dst)], axis=0)
    ex_ref[...] = dot(stacked, e_ref[...])
    carry = dot(paired(total), e_ref[...])[0:1]
    return z, step, cum, cum.T, carry


def taps_of(c, width, vtaps_ref, staps_ref):
    ref, at = (vtaps_ref, c) if c.start < width else (staps_ref, slice(c.start - width, c.stop - width))
    return lambda s: ref[K - 1 - s : K - s, at]


def lead_kernel(
    tokens_ref, go_ref, aux_ref, pg_ref, gate_w, value_w, state_w, step_w, out_w,
    vtaps_ref, staps_ref, vbias_ref, sbias_ref, heads_ref, skip_ref, ng_ref, e_ref, tri_ref,
    normed_ref, gate_ref, vs_ref, z_ref, gno_ref, y_ref, act_ref, pre_ref, stat_ref, sin_ref,
    ext_ref, state_ref, ex_ref, sum_ref, lane_ref,
):
    rows, width = gate_ref.shape
    chunks = range(rows // T)

    @pl.when(pl.program_id(0) % (SEQ_LEN // rows) == 0)
    def _():
        state_ref[...] = jnp.zeros_like(state_ref)
        ext_ref[0:8, :] = jnp.zeros_like(ext_ref[0:8, :])

    part = 32
    for lo in range(0, rows, part):
        hidden = tokens_ref[lo : lo + part, :].astype(f32)
        inv = lax.rsqrt(jnp.mean(hidden * hidden, axis=1, keepdims=True) + eps_value)
        for k in range(pg_ref.shape[0]):
            c = slice(k * LANES, (k + 1) * LANES)
            normed_ref[lo : lo + part, c] = (hidden[:, c] * inv * pg_ref[k : k + 1, :]).astype(bf16)
    z = dot_nt(normed_ref[...], step_w[...])
    z_ref[...] = jnp.zeros_like(z_ref)
    z_ref[:, : z.shape[1]] = z
    z_ref[:, HALF : HALF + z.shape[1]] = z
    raw = dot(normed_ref[...], state_w[...])
    ext_ref[8:, width:] = raw
    vs_ref[:, width:] = raw.astype(bf16)
    at = [pl.ds(k * T, T) for k in chunks]
    bias, rate = head_rows(heads_ref, lane_ref)
    aux = [aux_ref[k].T for k in chunks]
    terms = [
        head_terms(z_ref.at[at[k]], bias, rate, aux[k], tri_ref, e_ref, ex_ref.at[k])
        for k in chunks
    ]
    keep = [
        [jnp.broadcast_to(aux[k][:, s : s + 1], (T, LANES)) for s in range(K - 1)] for k in chunks
    ]

    def activate(c, k):
        lo = 8 + k * T
        tap, shift = taps_of(c, width, vtaps_ref, staps_ref), c.start // LANES
        if c.start < width:
            pre = vbias_ref[shift : shift + 1, :]
        else:
            pre = sbias_ref[shift - width // LANES : shift - width // LANES + 1, :]
        pre = pre + tap(0) * ext_ref[lo : lo + T, c]
        for s in range(1, K):
            pre = pre + tap(s) * (ext_ref[lo - s : lo - s + T, c] * keep[k][s - 1])
        half = 0.5 * pre
        act = half + half * jnp.tanh(half)
        act_bf = act.astype(bf16)
        pre_ref[at[k], c] = pre.astype(bf16)
        act_ref[at[k], c] = act_bf
        return act, act_bf

    row = lax.broadcasted_iota(jnp.int32, (T, T), 0)
    col = lax.broadcasted_iota(jnp.int32, (T, T), 1)
    b_flip, c_mats, scores, fades = [], [], [], []
    for k in chunks:
        _, b_mat = activate(slice(width, width + N), k)
        _, c_mat = activate(slice(width + N, width + 2 * N), k)
        b_flip.append(b_mat.T)
        c_mats.append(c_mat)
        scores.append(dot_nt(c_mat, b_mat))
        same = (aux[k][:, 5:6] == aux_ref[k, 5:6, :]) & (row >= col)
        fades.append(jnp.where(same, 0.0, NEG))
    first = lax.broadcasted_iota(jnp.int32, (T, LANES), 1) < HALF
    sum_ref[...] = jnp.zeros_like(sum_ref)
    span = 2 * LANES if width % (2 * LANES) == 0 else LANES
    for lo in range(0, width, span):
        group = slice(lo, lo + span)
        raw = dot(normed_ref[...], value_w[:, group])
        ext_ref[8:, group] = raw
        vs_ref[:, group] = raw.astype(bf16)
        gates = dot(normed_ref[...], gate_w[:, group])
        gate_ref[:, group] = gates.astype(bf16)
        gnos = dot_nt(go_ref[...], out_w[group, :])
        gno_ref[:, group] = gnos.astype(bf16)
        for pair in range(lo // LANES, (lo + span) // LANES):
            c = slice(pair * LANES, (pair + 1) * LANES)
            inside = slice(pair * LANES - lo, (pair + 1) * LANES - lo)
            for k in chunks:
                _, _, cum, cum_t, carry = terms[k]
                r = slice(k * T, (k + 1) * T)
                act, act_bf = activate(c, k)
                xt_full = act_bf.astype(f32) * ex_ref[k, 0:T, c]
                xt = xt_full.astype(bf16)
                xd = (xt_full * ex_ref[k, T : 2 * T, c]).astype(bf16)
                mixes = []
                for h in (2 * pair, 2 * pair + 1):
                    decay = jnp.exp(fades[k] + (cum[:, h : h + 1] - cum_t[h : h + 1, :]))
                    mixes.append((scores[k] * decay).astype(bf16))
                zero = jnp.zeros_like(xt)
                blocks = [jnp.where(first, xt, zero), jnp.where(first, zero, xt)]
                state = state_ref[:, c]
                state_bf = state.astype(bf16)
                sin_ref[k, :, c] = state_bf
                y = dot(jnp.concatenate(mixes, axis=1), jnp.concatenate(blocks, axis=0))
                y = y + ex_ref[k, 2 * T : 3 * T, c] * dot(c_mats[k], state_bf)
                y_ref[r, c] = y
                state_ref[:, c] = state * carry[:, c] + dot(b_flip[k], xd)
                half = 0.5 * gates[r, inside]
                gated = (y + skip_ref[pair : pair + 1, :] * act) * (half + half * jnp.tanh(half))
                sum_ref[k, 0] += gated * gated
                sum_ref[k, 1] += gated * ng_ref[pair : pair + 1, :] * gnos[r, inside]
    for k in chunks:
        for s in range(2):
            stat_ref[k, s : s + 1, :] = jnp.sum(sum_ref[k, s].T, axis=0, keepdims=True)
    ext_ref[0:8, :] = ext_ref[rows : rows + 8, :]


def store_half(value, sent_ref, kept_ref):
    first = pl.program_id(0) < pl.num_programs(0) // 2

    @pl.when(first)
    def _():
        sent_ref[...] = value

    @pl.when(jnp.logical_not(first))
    def _():
        kept_ref[...] = value


def middle_kernel(
    _, gate_ref, gno_ref, y_ref, act_ref, stat_ref, skip_ref, ng_ref, out_w,
    gate_grad_ref, mix_ref, normed_ref, sent_ref, kept_ref, csum_ref,
):
    @pl.when(pl.program_id(0) == 0)
    def _():
        csum_ref[...] = jnp.zeros_like(csum_ref)

    for chunk in range(stat_ref.shape[0]):
        r = slice(chunk * T, (chunk + 1) * T)
        scale = jnp.broadcast_to(stat_ref[chunk, 0:1, :], (LANES, T)).T
        slope_scale = jnp.broadcast_to(stat_ref[chunk, 1:2, :], (LANES, T)).T
        for pair in range(gate_ref.shape[1] // LANES):
            c = slice(pair * LANES, (pair + 1) * LANES)
            gate = gate_ref[r, c].astype(f32)
            logistic = sigmoid(gate)
            swish = gate * logistic
            x = act_ref[r, c].astype(f32)
            gno = gno_ref[r, c].astype(f32)
            ssd = y_ref[r, c] + skip_ref[pair : pair + 1, :] * x
            gated = ssd * swish
            unit = gated * scale
            normed_ref[r, c] = (unit * ng_ref[pair : pair + 1, :]).astype(bf16)
            grad_gated = scale * (gno * ng_ref[pair : pair + 1, :]) - slope_scale * gated
            csum_ref[0:8, c] += sum_rows(gno * unit)
            grad_mix = grad_gated * swish
            grad_gate = grad_gated * ssd * (logistic + swish * (1.0 - logistic))
            gate_grad_ref[r, c] = grad_gate.astype(bf16)
            csum_ref[8:16, c] += sum_rows(grad_mix * x)
            mix_ref[r, c] = grad_mix.astype(bf16)

    store_half(dot(normed_ref[...], out_w[...]).astype(bf16), sent_ref, kept_ref)


def backward_kernel(
    mix_ref, y_ref, act_ref, pre_ref, vs_ref, z_ref, sin_ref, aux_ref,
    vtaps_ref, staps_ref, heads_ref, skip_ref, e_ref, er_ref, tri_ref, triu_ref,
    grad_ref, csum_ref,
    back_ref, ext_ref, ex_ref, xd_ref, gd_ref, through_ref, lane_ref, part_ref,
):
    width = mix_ref.shape[1]

    @pl.when((pl.program_id(0) == 0) & (pl.program_id(1) == 0))
    def _():
        csum_ref[...] = jnp.zeros_like(csum_ref)

    @pl.when(pl.program_id(1) == 0)
    def _():
        back_ref[...] = jnp.zeros_like(back_ref)
        ext_ref[T : T + 8, :] = jnp.zeros_like(ext_ref[T : T + 8, :])

    bias, rate = head_rows(heads_ref, lane_ref)
    aux = aux_ref[0].T
    z, step, cum, cum_t, carry = head_terms(z_ref, bias, rate, aux, tri_ref, e_ref, ex_ref)
    keep = [jnp.broadcast_to(aux[:, 5 + s : 6 + s], (T, LANES)) for s in range(1, K)]
    b_mat = act_ref[:, width : width + N]
    c_mat = act_ref[:, width + N : width + 2 * N]
    scores_t = dot_nt(b_mat, c_mat)
    row = lax.broadcasted_iota(jnp.int32, (T, T), 0)
    col = lax.broadcasted_iota(jnp.int32, (T, T), 1)
    same = (aux[:, 5:6] == aux_ref[0, 5:6, :]) & (row <= col)
    fade = jnp.where(same, 0.0, NEG)
    lane = lax.broadcasted_iota(jnp.int32, (T, LANES), 1)
    first = lane < HALF
    back_bf = back_ref[...].astype(bf16)

    def conv_back(grad_pre, c):
        ext_ref[0:T, c] = grad_pre
        raw = vs_ref[:, c].astype(f32)
        tap = taps_of(c, width, vtaps_ref, staps_ref)
        grad_raw = tap(0) * grad_pre
        csum_ref[8 * (K - 1) : 8 * K, c] += sum_rows(grad_pre * raw)
        csum_ref[8 * K : 8 * K + 8, c] += sum_rows(grad_pre)
        for s in range(1, K):
            moved = ext_ref[s : s + T, c] * keep[s - 1]
            grad_raw = grad_raw + tap(s) * moved
            csum_ref[8 * (K - 1 - s) : 8 * (K - s), c] += sum_rows(moved * raw)
        return grad_raw

    def slope(c):
        pre = pre_ref[:, c].astype(f32)
        logistic = sigmoid(pre)
        return logistic * (1.0 + pre * (1.0 - logistic))

    def through_of(value):
        high, low = two_terms(sum_rows(value))
        through = dot(high, er_ref[...]) + dot(low, er_ref[...])
        return jnp.broadcast_to(jnp.sum(through, axis=0, keepdims=True), (8, LANES))

    grad_scores = jnp.zeros((T, T), f32)
    through_ref[...] = through_of(sin_ref[0].astype(f32) * back_ref[...] * carry)
    for pair in range(width // LANES):
        c = slice(pair * LANES, (pair + 1) * LANES)
        x = act_ref[:, c].astype(f32)
        y = y_ref[:, c]
        g = mix_ref[:, c]
        grad_mix = g.astype(f32)
        step_x = ex_ref[0:T, c]
        dend_x = ex_ref[T : 2 * T, c]
        gd_ref[:, c] = (grad_mix * ex_ref[2 * T : 3 * T, c]).astype(bf16)
        xt_full = x * step_x
        xt = xt_full.astype(bf16)
        xd_ref[:, c] = (xt_full * dend_x).astype(bf16)
        zero = jnp.zeros_like(g)
        g_blocks = jnp.concatenate([jnp.where(first, g, zero), jnp.where(first, zero, g)], axis=0)
        x_blocks = jnp.concatenate([jnp.where(first, xt, zero), jnp.where(first, zero, xt)], axis=0)
        products = dot_nt(x_blocks, g)
        mixes = []
        for k, h in enumerate((2 * pair, 2 * pair + 1)):
            decay = jnp.exp(fade + (cum_t[h : h + 1, :] - cum[:, h : h + 1]))
            mixes.append((scores_t * decay).astype(bf16))
            grad_scores = grad_scores + products[k * T : (k + 1) * T] * decay
        u_in = dot(jnp.concatenate(mixes, axis=1), g_blocks)
        u_far = dend_x * dot(b_mat, back_bf[:, c])
        u = u_in + u_far
        y_far = ex_ref[2 * T : 3 * T, c] * dot(c_mat, sin_ref[0, :, c])
        xt_wide = xt.astype(f32)
        part_ref[0, :, c], part_ref[1, :, c] = two_terms(grad_mix * (y - y_far) - xt_wide * u_in)
        part_ref[2, :, c] = (grad_mix * y_far).astype(bf16)
        part_ref[3, :, c] = (xt_wide * u_far).astype(bf16)
        part_ref[4, :, c] = (x * u).astype(bf16)
        grad_value = step_x * u + skip_ref[pair : pair + 1, :] * grad_mix
        grad_ref[:, c] = conv_back(grad_value * slope(c), c).astype(bf16)

    gs_bf = grad_scores.astype(bf16)
    grad_b = dot(gs_bf, c_mat) + dot_nt(xd_ref[...], back_bf)
    grad_c = dot_tn(gs_bf, b_mat) + dot_nt(gd_ref[...], sin_ref[0])
    for k, grad in enumerate((grad_b, grad_c)):
        c = slice(width + k * N, width + (k + 1) * N)
        grad_ref[:, c] = conv_back(grad * slope(c), c).astype(bf16)
    ext_ref[T : T + 8, :] = ext_ref[0:8, :]

    by_head = [dot(part_ref[k], er_ref[...]) for k in range(5)]
    col_far, direct = by_head[3:]
    high, low = two_terms(by_head[0] + by_head[1] + by_head[2])
    grad_acc = through_ref[0:1, :] + (dot(triu_ref[...], high) + dot(triu_ref[...], low))
    high, low = two_terms(col_far)
    grad_acc = grad_acc + (dot(tri_ref[...], high) + dot(tri_ref[...], low)) - col_far
    grad_step = direct + grad_acc * rate
    grad_z = grad_step * sigmoid(z)
    csum_ref[8 * (K + 1) : 8 * (K + 2), 0:LANES] += sum_rows(grad_z)
    csum_ref[8 * (K + 1) : 8 * (K + 2), LANES : 2 * LANES] += sum_rows(grad_acc * step)
    grad_ref[:, width + 2 * N :] = grad_z.astype(bf16)

    new_back = back_ref[...] * carry + dot_tn(c_mat, gd_ref[...])
    back_ref[...] = new_back


def bits_of(size):
    return [1 << k for k in range(size.bit_length() - 1)] if size & (size - 1) == 0 else None


def swap(value, axis, size, bit):
    return lax.ppermute(value, axis, [(i, i ^ bit) for i in range(size)])


def block_of(rows):
    return max(b for b in range(16, 513, 16) if rows % b == 0)


def place(buffer, value, slot, dtype, mixed=False):
    rows, width = value.shape
    block = rows // 2 if mixed else block_of(rows)
    count = rows // block
    where = (lambda i, s: (2 * i + s[0], 0)) if mixed else (lambda i, s: (s[0] * count + i, 0))

    def kernel(slot_ref, value_ref, *refs):
        refs[-1][...] = value_ref[...].astype(dtype)

    out = jax.ShapeDtypeStruct((2 * rows, width), dtype)
    given = () if buffer is None else (buffer,)
    return pl.pallas_call(
        kernel,
        grid_spec=pltpu.PrefetchScalarGridSpec(
            num_scalar_prefetch=1,
            grid=(count,),
            in_specs=[pl.BlockSpec((block, width), lambda i, s: (i, 0))]
            + [pl.BlockSpec(memory_space=pl.ANY) for _ in given],
            out_specs=pl.BlockSpec((block, width), where),
        ),
        out_shape=out,
        input_output_aliases={2: 0} if given else {},
        name="place",
    )(jnp.reshape(slot, (1,)).astype(jnp.int32), value, *given)


def join(value, other, upper):
    rows, width = value.shape
    block = block_of(rows)
    count = rows // block

    def kernel(upper_ref, value_ref, other_ref, out_ref):
        mine = pl.program_id(0) == upper_ref[0]

        @pl.when(mine)
        def _():
            out_ref[...] = value_ref[...]

        @pl.when(jnp.logical_not(mine))
        def _():
            out_ref[...] = other_ref[...]

    return pl.pallas_call(
        kernel,
        grid_spec=pltpu.PrefetchScalarGridSpec(
            num_scalar_prefetch=1,
            grid=(2, count),
            in_specs=[
                pl.BlockSpec((block, width), lambda h, i, u: (jnp.where(h == u[0], i, 0), 0)),
                pl.BlockSpec((block, width), lambda h, i, u: (jnp.where(h == u[0], 0, i), 0)),
            ],
            out_specs=pl.BlockSpec((block, width), lambda h, i, u: (h * count + i, 0)),
        ),
        out_shape=jax.ShapeDtypeStruct((2 * rows, width), value.dtype),
        name="join",
    )(jnp.reshape(upper, (1,)).astype(jnp.int32), value, other)


def add_parts(parts, start, rows):
    total = None
    for value, base in parts:
        piece = lax.dynamic_slice_in_dim(value, base + start, rows, 0).astype(f32)
        total = piece if total is None else total + piece
    return total


def scatter_halves(kept, sent, axis, size):
    bits = bits_of(size)
    if size != 4:
        quarter = (2, kept.shape[0] // 2, kept.shape[1])
        value = jnp.stack([kept.reshape(quarter), sent.reshape(quarter)], axis=1)
        value = value.reshape(2 * kept.shape[0], kept.shape[1])
        return lax.psum_scatter(value, axis, scatter_dimension=0, tiled=True).astype(f32)
    other = swap(sent, axis, size, bits[0])
    return scatter_parts([(kept, 0), (other, 0)], axis, size, bits[1:])


def scatter_sum(value, axis, size):
    bits = bits_of(size)
    if bits is None:
        return lax.psum_scatter(value, axis, scatter_dimension=0, tiled=True).astype(f32)
    return scatter_parts([(value, 0)], axis, size, bits)


def scatter_parts(parts, axis, size, bits):
    index = lax.axis_index(axis)
    value = parts[0][0]
    rows = value.shape[0]
    for bit in bits:
        upper = (index // bit) % 2
        rows = rows // 2
        sent = add_parts(parts, (1 - upper) * rows, rows).astype(value.dtype)
        other = swap(sent, axis, size, bit)
        parts = [(part, base + upper * rows) for part, base in parts] + [(other, 0)]
    return add_parts(parts, 0, rows)


def gather_rows(value, axis, size, dtype, mixed=False):
    index = lax.axis_index(axis)
    bits = bits_of(size)
    if bits is None:
        return lax.all_gather(value, axis, axis=0, tiled=True).astype(dtype)
    for bit in bits[::-1]:
        other = swap(value, axis, size, bit)
        upper = (index // bit) % 2
        if bit == bits[0]:
            buffer = place(None, value, upper, dtype, mixed)
            value = place(buffer, other, 1 - upper, dtype, mixed)
        else:
            value = join(value, other, upper)
    return value.astype(dtype)


def reduce_rows(value, axis, size, dtype):
    part = scatter_sum(value, axis, size).astype(value.dtype)
    return gather_rows(part, axis, size, dtype)


def butterfly(value, axis, size):
    bits = bits_of(size)
    if bits is None:
        return lax.psum(value, axis)
    for bit in bits:
        value = value + swap(value, axis, size, bit)
    return value


def token_aux(segments):
    count = segments.shape[0]
    seg = segments.astype(f32)
    position = jnp.arange(count, dtype=jnp.int32) % SEQ_LEN
    columns = []
    lifted = []
    for s in range(1, K):
        before = jnp.concatenate([jnp.zeros((s,), f32), seg[:-s]])
        keep = ((position >= s) & (seg == before)).astype(f32)
        columns.append(keep)
        lifted.append(jnp.concatenate([keep[s:], jnp.zeros((s,), f32)]))
    chunked = seg.reshape(count // T, T)
    last = chunked[:, T - 1]
    starts = (jnp.arange(count // T, dtype=jnp.int32) * T) % SEQ_LEN == 0
    before = jnp.where(starts, -1.0, jnp.concatenate([jnp.zeros((1,), f32), last[:-1]]))
    columns.append((chunked == before[:, None]).astype(f32).reshape(count))
    columns.append((chunked == last[:, None]).astype(f32).reshape(count))
    columns.append(seg)
    rows = [row.reshape(count // T, T) for row in columns + lifted]
    return jnp.stack(rows + [rows[0]] * (16 - len(rows)), axis=1)


def group_kernel(
    _, gate_ref, packed_ref, normed_ref, gate_w, value_w, state_w, step_w,
    sent_ref, kept_ref, gain_ref, in_ref,
):
    weights = (value_w, state_w)
    steps = packed_ref[:, value_w.shape[1] + state_w.shape[1] :][:, : step_w.shape[0]]

    @pl.when(pl.program_id(0) == 0)
    def _():
        gain_ref[...] = jnp.zeros_like(gain_ref)

    model = in_ref.shape[1]
    part = model // 3 if model % 384 == 0 else model
    for lo in range(0, model, part):
        c = slice(lo, lo + part)
        total, at = dot_nt(gate_ref[...], gate_w[c, :]) + dot(steps, step_w[:, c]), 0
        for w in weights:
            total = total + dot_nt(packed_ref[:, at : at + w.shape[1]], w[c, :])
            at += w.shape[1]
        rounded = total.astype(bf16)
        in_ref[:, c] = rounded
        gain_ref[:, c] += sum_rows(rounded.astype(f32) * normed_ref[:, c].astype(f32))
    store_half(in_ref[...], sent_ref, kept_ref)


def on_device(
    tokens_in, segments, pre_gain, gate_proj, value_proj, state_proj, step_proj, conv_value,
    conv_value_bias, conv_state, conv_state_bias, step_bias, decay_log, skip_gain, norm_gain,
    out_proj, grad_out, *, n_dp, n_tensor,
):
    tokens, model = tokens_in.shape
    width = gate_proj.shape[1]
    heads = step_proj.shape[1]
    head_width = width // heads
    chunks = tokens // T
    seqs = tokens // SEQ_LEN
    per_seq = SEQ_LEN // T
    wide = width + 2 * N
    full = wide + LANES
    inner_width = width * n_tensor

    aux = token_aux(segments)

    projections = (gate_proj, value_proj, state_proj, step_proj.T)
    block = tokens // 4
    lead = 2 * T
    by_rows = lambda columns: pl.BlockSpec((lead, columns), lambda i: (i, 0))
    by_chunks = lambda *shape: pl.BlockSpec((lead // T,) + shape, lambda i: (i, 0, 0))
    held = lambda value: pl.BlockSpec(
        value.shape, lambda i: (0,) * value.ndim, pipeline_mode=pl.Buffered(1)
    )
    vbias = conv_value_bias.reshape(width // LANES, LANES)
    sbias = conv_state_bias.reshape(2 * N // LANES, LANES)
    head_pair = jnp.stack([step_bias, decay_log])
    decay_rate = -jnp.exp(decay_log)
    skip = jnp.repeat(skip_gain, head_width).reshape(width // LANES, LANES)
    gain = norm_gain.reshape(width // LANES, LANES)
    lanes = np.arange(LANES)
    owner = np.arange(width) // head_width
    expand = jnp.asarray(lanes[:, None] % HALF == owner[None, :], bf16)
    reduce = jnp.asarray(owner[:, None] == lanes[None, :], bf16)
    rows = np.arange(T)
    tri = jnp.asarray(rows[:, None] >= rows[None, :], bf16)
    triu = jnp.asarray(rows[:, None] <= rows[None, :], bf16)

    def at(block, index):
        return pl.BlockSpec(block, index)

    def whole(value):
        return pl.BlockSpec(value.shape, lambda i, j: (0,) * value.ndim, pipeline_mode=pl.Buffered(1))

    sds = jax.ShapeDtypeStruct
    pg_rows = pre_gain.reshape(model // LANES, LANES)
    consts = (pg_rows,) + projections + (out_proj, conv_value, conv_state, vbias, sbias)
    consts += (head_pair, skip, gain, expand, tri)
    normed, gate_raw, vs_raw, z_raw, grad_normed_out, y, act, pre, stat, sin = pl.pallas_call(
        lead_kernel,
        grid=(tokens // lead,),
        in_specs=[by_rows(model), by_rows(model), by_chunks(16, T)]
        + [held(v) for v in consts],
        out_specs=[by_rows(c) for c in (model, width, wide, LANES, width, width, wide, wide)]
        + [by_chunks(2, T), by_chunks(N, width)],
        out_shape=[
            sds((tokens, model), bf16), sds((tokens, width), bf16), sds((tokens, wide), bf16),
            sds((tokens, LANES), f32), sds((tokens, width), bf16), sds((tokens, width), f32),
            sds((tokens, wide), bf16), sds((tokens, wide), bf16), sds((chunks, 2, T), f32),
            sds((chunks, N, width), bf16),
        ],
        scratch_shapes=[
            pltpu.VMEM((lead + 8, wide), f32), pltpu.VMEM((N, width), f32),
            pltpu.VMEM((lead // T, 3 * T, width), f32), pltpu.VMEM((lead // T, 2, T, LANES), f32),
            pltpu.VMEM((8, LANES), f32),
        ],
        name="lead",
    )(tokens_in, grad_out, aux, *consts)

    if n_tensor == 4:
        others = [swap(stat, "tensor", n_tensor, bit) for bit in (1, 2, 3)]
        stat = (stat + others[0]) + (others[1] + others[2])
    else:
        stat = butterfly(stat, "tensor", n_tensor)
    scale = lax.rsqrt(stat[:, 0] / inner_width + eps_value)
    slope_scale = scale * scale * scale * stat[:, 1] / inner_width
    scales = jnp.stack([scale, slope_scale], axis=1)
    steps = tokens // block
    upper = lax.axis_index("tensor") % 2 if n_tensor == 4 else 0
    upper = jnp.reshape(jnp.asarray(upper, jnp.int32), (1,))
    turn = lambda i, u: jnp.where(i < 2, 2 * i + 1 - u[0], 2 * i - 4 + u[0])
    turned = lambda columns: pl.BlockSpec((block, columns), lambda i, u: (turn(i, u), 0))
    kept_spec = lambda columns: pl.BlockSpec(
        (block, columns), lambda i, u: (jnp.maximum(i - steps // 2, 0), 0)
    )
    sent_spec = lambda columns: pl.BlockSpec(
        (block, columns), lambda i, u: (jnp.minimum(i, steps // 2 - 1), 0)
    )
    fixed = lambda rows, columns: pl.BlockSpec((rows, columns), lambda i, u: (0, 0))
    still = lambda value: pl.BlockSpec(
        value.shape, lambda i, u: (0,) * value.ndim, pipeline_mode=pl.Buffered(1)
    )
    halves = [sds((tokens // 2, model), bf16)] * 2
    gate_bf, mix, normed_out, sent, kept, gate_sums = pl.pallas_call(
        middle_kernel,
        grid_spec=pltpu.PrefetchScalarGridSpec(
            num_scalar_prefetch=1,
            grid=(steps,),
            in_specs=[turned(width)] * 4
            + [pl.BlockSpec((block // T, 2, T), lambda i, u: (turn(i, u), 0, 0))]
            + [still(skip), still(gain), still(out_proj)],
            out_specs=[turned(width)] * 3
            + [sent_spec(model), kept_spec(model), fixed(16, width)],
        ),
        out_shape=[sds((tokens, width), bf16)] * 3 + halves + [sds((16, width), f32)],
        name="middle",
    )(upper, gate_raw, grad_normed_out, y, act, scales, skip, gain, out_proj)
    grad_out_proj = dot_tn(normed_out, grad_out).astype(bf16)
    grad_gate_proj = dot_tn(normed, gate_bf).astype(bf16)
    grad_out_proj = lax.psum(grad_out_proj, "dp")
    grad_out_proj = grad_out_proj.astype(f32)
    grad_gate_proj = reduce_rows(grad_gate_proj, "dp", n_dp, f32)

    start = lax.axis_index("tensor") * (tokens // n_tensor)
    own = lambda v: lax.dynamic_slice_in_dim(v, start, tokens // n_tensor, 0)
    branch = scatter_halves(kept, sent, "tensor", n_tensor)
    own_hidden = own(tokens_in).astype(f32)
    block_out = (own_hidden + branch).astype(bf16)
    if n_tensor == 4:
        block_out = gather_rows(block_out, "tensor", n_tensor, bf16, mixed=True)
    else:
        block_out = lax.all_gather(block_out, "tensor", axis=0, tiled=True)

    consts = (conv_value, conv_state, head_pair, skip, expand, reduce, tri, triu)
    bwd = lambda i, j: (i * per_seq + per_seq - 1 - j, 0)
    bwd3 = lambda i, j: (i * per_seq + per_seq - 1 - j, 0, 0)
    packed, csum = pl.pallas_call(
        backward_kernel,
        grid=(seqs, per_seq),
        in_specs=[
            at((T, width), bwd), at((T, width), bwd), at((T, wide), bwd), at((T, wide), bwd),
            at((T, wide), bwd), at((T, LANES), bwd), at((1, N, width), bwd3),
            at((1, 16, T), bwd3),
        ] + [whole(v) for v in consts],
        out_specs=[
            at((T, full), bwd), pl.BlockSpec((8 * (K + 2), wide), lambda i, j: (0, 0)),
        ],
        out_shape=[sds((tokens, full), bf16), sds((8 * (K + 2), wide), f32)],
        scratch_shapes=[
            pltpu.VMEM((N, width), f32), pltpu.VMEM((T + 8, wide), f32),
            pltpu.VMEM((3 * T, width), f32), pltpu.VMEM((T, width), bf16),
            pltpu.VMEM((T, width), bf16), pltpu.VMEM((8, LANES), f32),
            pltpu.VMEM((8, LANES), f32), pltpu.VMEM((5, T, width), bf16),
        ],
        name="ssd_backward",
    )(mix, y, act, pre, vs_raw, z_raw, sin, aux, *consts)

    grad_value_proj = dot_tn(normed, packed[:, :width]).astype(bf16)
    grad_state_proj = dot_tn(normed, packed[:, width:wide]).astype(bf16)
    grad_step_proj = dot_tn(packed[:, wide:], normed)[:heads]
    sent, kept, gain_part = pl.pallas_call(
        group_kernel,
        grid_spec=pltpu.PrefetchScalarGridSpec(
            num_scalar_prefetch=1,
            grid=(steps,),
            in_specs=[turned(width), turned(full), turned(model)]
            + [still(w) for w in projections],
            out_specs=[sent_spec(model), kept_spec(model), fixed(8, model)],
            scratch_shapes=[pltpu.VMEM((block, model), bf16)],
        ),
        out_shape=halves + [sds((8, model), f32)],
        name="group_in",
    )(upper, gate_bf, packed, normed, *projections)
    gate_sums = jnp.pad(gate_sums, ((0, 0), (0, 2 * N)))
    sums = jnp.sum(jnp.concatenate([csum, gate_sums]).reshape(K + 4, 8, wide), axis=1)
    gain_part = jnp.sum(gain_part, axis=0) / pre_gain

    grad_value_proj = reduce_rows(grad_value_proj, "dp", n_dp, f32)

    grad_normed = scatter_halves(kept, sent, "tensor", n_tensor)
    tokens_late, _ = lax.optimization_barrier((tokens_in, kept))
    own_hidden = own(tokens_late).astype(f32)
    own_inv = lax.rsqrt(jnp.mean(own_hidden * own_hidden, axis=1, keepdims=True) + eps_value)
    weighted = pre_gain * grad_normed
    grad_hidden = own_inv * weighted - own_hidden * (own_inv * own_inv * own_inv) * jnp.mean(
        weighted * own_hidden, axis=1, keepdims=True
    )
    grad_in = (own(grad_out).astype(f32) + grad_hidden).astype(bf16)
    grad_in = lax.all_gather(grad_in, "tensor", axis=0, tiled=True)

    gain_rows = model // (2 * N)
    extra = jnp.concatenate([sums[:, width:], gain_part.reshape(gain_rows, 2 * N)], axis=0)
    unit = n_tensor * math.lcm(16, model // math.gcd(model, 2 * N))
    gap = -(model + extra.shape[0]) % unit
    extra = jnp.pad(extra, ((0, gap), (0, 0))).astype(bf16)
    shared = jnp.concatenate([grad_state_proj, extra], axis=0)
    shared = scatter_sum(shared, "tensor", n_tensor).astype(bf16)
    small = jnp.concatenate([jnp.pad(sums, ((0, 0), (0, model - wide))), grad_step_proj], axis=0)
    part = shared.shape[0]
    flat = part * 2 * N // model
    both = jnp.concatenate([shared.reshape(flat, model), small.astype(bf16)], axis=0)
    both = butterfly(both, "dp", n_dp)
    shared, small = both[:flat].reshape(part, 2 * N), both[flat:].astype(f32)
    shared = gather_rows(shared, "tensor", n_tensor, bf16)
    grad_state_proj = shared[:model].astype(f32)
    state_sums = shared[model : model + K + 4].astype(f32)
    grad_pre_gain = shared[model + K + 4 : model + K + 4 + gain_rows].reshape(model).astype(f32)
    sums = small[: K + 4]
    grad_step_proj = small[K + 4 :].T
    grad_skip = jnp.sum(sums[K + 3, :width].reshape(heads, head_width), axis=1)
    return (
        block_out,
        grad_in,
        grad_pre_gain,
        grad_gate_proj,
        grad_value_proj,
        grad_state_proj,
        grad_step_proj,
        sums[:K, :width],
        sums[K, :width],
        state_sums[:K],
        state_sums[K],
        sums[K + 1, :heads],
        sums[K + 1, LANES : LANES + heads] * decay_rate,
        grad_skip,
        sums[K + 2, :width],
        grad_out_proj,
    )


def solution(mesh):
    t = P("tensor")
    cols = P(None, "tensor")
    in_specs = (
        P("dp", None), P("dp"), P(), cols, cols, P(), cols, cols, t, P(), P(), t, t, t, t,
        P("tensor", None), P("dp", None),
    )
    out_specs = (
        P("dp", None), P("dp", None), P(), cols, cols, P(), cols, cols, t, P(), P(), t, t, t, t,
        P("tensor", None),
    )
    n_dp, n_tensor = mesh.shape["dp"], mesh.shape["tensor"]

    def body(*args):
        return on_device(*args, n_dp=n_dp, n_tensor=n_tensor)

    return jax.shard_map(body, mesh=mesh, in_specs=in_specs, out_specs=out_specs, check_vma=False)
```

profile of v0, /device:TPU:0, one launch (start us, length us, event | category | flops | bytes accessed | tf_op | source)
XLA Modules:
  0.0 488.6 jit_solution(7734657549626154363)
XLA Ops:
  14.6 48.7 %lead.1 = (bf16[2048,1536]{1,0:T(8,128)(2,1)}, bf16[2048,768]{1,0:T(8,128)(2,1)}, bf16[2048,1024]{1,0:T(8,128)(2,1)}, f32[2048,128]{1,0:T(8,128)}, bf16[2048,768...) custom-call(bf16[2048,1536]{1,0:T(8,128)(2,1)} %tokens_ref.1, ...), custom_call_target="tpu_custom_call" | custom-call | tf_op jit(solution)/shard_map/lead/pallas_call | solution.py:595
  71.1 18.9 %middle.1 = (bf16[2048,768]{1,0:T(8,128)(2,1)}, bf16[2048,768]{1,0:T(8,128)(2,1)}, bf16[2048,768]{1,0:T(8,128)(2,1)}, bf16[1024,1536]{1,0:T(8,128)(2,1)}, bf16[1024,1536]{1,0:T(8,128)(2,1)}, /*index=5*/f32[16,768]{1,0:T(8,128)}) custom-call(s32[1]{0:T(128)} %bitcast.2._.slot_ref, bf16[2048,768]{1,0:T(8,128)(2,1)} %get-tuple-element.38.gate_ref, ...), custom_call_target="tpu_custom_call" | custom-call | tf_op jit(solution)/shard_map/middle/pallas_call | solution.py:640
  90.1 47.2 %ssd_backward.1 = (bf16[2048,1152]{1,0:T(8,128)(2,1)}, f32[48,1024]{1,0:T(8,128)}) custom-call(bf16[2048,768]{1,0:T(8,128)(2,1)} %get-tuple-element.46.mix_ref, f32[2048,768]{1,0:T(8,128)} %get-tuple-element.40.y_ref, bf16[2048,1024]{1,0:T(8,128)(2,1)} %get-tuple-element.41.act_ref, bf16[2048,1024]{1,0:T(8,128)(2,1)} %get-tuple-element.47.pre_ref, ...), custom_call_target="tpu_custom_call" | custom-call | tf_op jit(solution)/shard_map/ssd_backward/pallas_call | solution.py:673
  137.3 20.6 %group_in.1 = (bf16[1024,1536]{1,0:T(8,128)(2,1)}, bf16[1024,1536]{1,0:T(8,128)(2,1)}, f32[8,1536]{1,0:T(8,128)}) custom-call(s32[1]{0:T(128)} %bitcast.2._.slot_ref, bf16[2048,768]{1,0:T(8,128)(2,1)} %get-tuple-element.45.gate_ref, bf16[2048,1152]{1,0:T(8,128)(2,1)} %get-tuple-element.51.packed_ref, bf16[2048,1536]{1,0:T(8,128)(2,1)} %get-tuple-element.52.normed_ref, ...), custom_call_target="tpu_custom_call" | custom-call | tf_op jit(solution)/shard_map/group_in/pallas_call | solution.py:697
  158.0 5.8 %collective-permute-done.7 = bf16[1024,1536]{1,0:T(8,128)(2,1)S(1)} collective-permute-done((bf16[1024,1536]{1,0:T(8,128)(2,1)}, bf16[1024,1536]{1,0:T(8,128)(2,1)S(1)}, u32[]{:S(2)}, u32[]{:S(2)}) %collective-permute-start.7) | collective-permute-done | bytes 3145760 | tf_op jit(solution)/shard_map/ppermute | solution.py:364
  163.9 4.1 add_convert_fusion
  168.6 9.3 %convolution_convert_fusion = bf16[768,1536]{1,0:T(8,128)(2,1)} fusion(bf16[2048,768]{1,0:T(8,128)(2,1)S(1)} %copy-done.17, bf16[2048,1536]{1,0:T(8,128)(2,1)} %go_ref.1), kind=kOutput, calls=%fused_computation.3 | convolution fusion | flops 4833017856 | bytes 11796480 | tf_op jit(solution)/shard_map/dot_general | solution.py:33
  178.3 26.4 %collective-permute-done.8 = bf16[512,1536]{1,0:T(8,128)(2,1)} collective-permute-done((bf16[512,1536]{1,0:T(8,128)(2,1)}, bf16[512,1536]{1,0:T(8,128)(2,1)}, u32[]{:S(2)}, u32[]{:S(2)}) %collective-permute-start.8) | collective-permute-done | bytes 1572896 | tf_op jit(solution)/shard_map/ppermute | solution.py:364
  204.7 3.6 fusion
  208.3 5.0 %fusion.4 = bf16[512,1536]{1,0:T(8,128)(2,1)} fusion(bf16[512,1536]{1,0:T(8,128)(2,1)} %collective-permute-done.8, f32[512]{0:T(512)S(1)} %get-tuple-element.76, f32[512]{0:T(512)S(1)} %get-tuple-element.75, f32[1536]{0:T(1024)S(1)} %copy-done.13, f32[512]{0:T(512)S(1)} %get-tuple-element.74, bf16[2048,1536]{1,0:T(8,128)(2,1)} %go_ref.1, s32[]{:T(128)S(6)} %select_n.181, ...), kind=kLoop, calls=%fused_computation.10 | loop fusion | flops 11010048 | bytes 9449480 | tf_op jit(solution)/shard_map/convert_element_type | solution.py:724
  213.4 5.0 %convolution_convert_fusion.3 = bf16[1536,256]{1,0:T(8,128)(2,1)S(1)} fusion(bf16[2048,1536]{1,0:T(8,128)(2,1)} %get-tuple-element.52.normed_ref, bf16[2048,1152]{1,0:T(8,128)(2,1)} %get-tuple-element.51.packed_ref), kind=kOutput, calls=%fused_computation.17 | convolution fusion | flops 1611005952 | bytes 8126464 | tf_op jit(solution)/shard_map/dot_general | solution.py:33
  219.2 8.2 %convolution_convert_fusion.1 = bf16[1536,768]{1,0:T(8,128)(2,1)S(1)} fusion(bf16[2048,1536]{1,0:T(8,128)(2,1)S(1)} %bitcast.54, bf16[2048,1152]{1,0:T(8,128)(2,1)} %get-tuple-element.51.packed_ref), kind=kOutput, calls=%fused_computation.4 | convolution fusion | flops 4833017856 | bytes 11796480 | tf_op jit(solution)/shard_map/dot_general | solution.py:33
  230.8 5.5 %convolution_convert_fusion.2 = bf16[1536,768]{1,0:T(8,128)(2,1)S(1)} fusion(bf16[2048,1536]{1,0:T(8,128)(2,1)S(1)} %bitcast.54, bf16[2048,768]{1,0:T(8,128)(2,1)S(1)} %copy-done.3), kind=kOutput, calls=%fused_computation.5 | convolution fusion | flops 4833017856 | bytes 11796480 | tf_op jit(solution)/shard_map/dot_general | solution.py:33
  242.5 49.8 %collective-permute-done.4 = bf16[512,1536]{1,0:T(8,128)(2,1)S(1)} collective-permute-done((bf16[512,1536]{1,0:T(8,128)(2,1)S(1)}, bf16[512,1536]{1,0:T(8,128)(2,1)S(1)}, u32[]{:S(2)}, u32[]{:S(2)}) %collective-permute-start.4) | collective-permute-done | bytes 1572896 | tf_op jit(solution)/shard_map/ppermute | solution.py:364
  292.4 3.8 add_convert_fusion.1.value_ref
  311.6 7.0 %collective-permute-done.23 = bf16[384,768]{1,0:T(8,128)(2,1)S(1)} collective-permute-done((bf16[384,768]{1,0:T(8,128)(2,1)S(1)}, bf16[384,768]{1,0:T(8,128)(2,1)S(1)}, u32[]{:S(2)}, u32[]{:S(2)}) %collective-permute-start.23) | collective-permute-done | bytes 589856 | tf_op jit(solution)/shard_map/ppermute | solution.py:364
  323.1 19.1 %collective-permute-done.12 = bf16[92,1536]{1,0:T(8,128)(2,1)S(1)} collective-permute-done((bf16[92,1536]{1,0:T(8,128)(2,1)S(1)}, bf16[92,1536]{1,0:T(8,128)(2,1)S(1)}, u32[]{:S(2)}, u32[]{:S(2)}) %collective-permute-start.12) | collective-permute-done | bytes 282656 | tf_op jit(solution)/shard_map/ppermute | solution.py:364
  343.8 3.7 join.6.value_ref
  350.9 13.2 %collective-permute-done.13 = bf16[92,1536]{1,0:T(8,128)(2,1)} collective-permute-done((bf16[92,1536]{1,0:T(8,128)(2,1)S(1)}, bf16[92,1536]{1,0:T(8,128)(2,1)}, u32[]{:S(2)}, u32[]{:S(2)}) %collective-permute-start.13) | collective-permute-done | bytes 282656 | tf_op jit(solution)/shard_map/ppermute | solution.py:364
  376.2 14.6 %collective-permute-done.25.other_ref = bf16[192,768]{1,0:T(8,128)(2,1)S(1)} collective-permute-done((bf16[192,768]{1,0:T(8,128)(2,1)S(1)}, bf16[192,768]{1,0:T(8,128)(2,1)S(1)}, u32[]{:S(2)}, u32[]{:S(2)}) %collective-permute-start.25) | collective-permute-done | bytes 294944 | tf_op jit(solution)/shard_map/ppermute | solution.py:364
  412.7 9.1 %collective-permute-done.20.other_ref = bf16[384,768]{1,0:T(8,128)(2,1)} collective-permute-done((bf16[384,768]{1,0:T(8,128)(2,1)}, bf16[384,768]{1,0:T(8,128)(2,1)}, u32[]{:S(2)}, u32[]{:S(2)}) %collective-permute-start.20) | collective-permute-done | bytes 589856 | tf_op jit(solution)/shard_map/ppermute | solution.py:364
  435.1 4.5 convert_element_type.283
  447.2 17.2 %collective-permute-done.21.value_ref = bf16[768,768]{1,0:T(8,128)(2,1)} collective-permute-done((bf16[768,768]{1,0:T(8,128)(2,1)}, bf16[768,768]{1,0:T(8,128)(2,1)}, u32[]{:S(2)}, u32[]{:S(2)}) %collective-permute-start.21) | collective-permute-done | bytes 1179680 | tf_op jit(solution)/shard_map/ppermute | solution.py:364
  475.0 5.9 %copy.49 = bf16[2048,1536]{1,0:T(8,128)(2,1)} copy(bf16[2048,1536]{1,0:T(8,128)(2,1)} %all-gather.2.cloned.1.call-done) | data formatting | bytes 12582912
  (170 shorter events, 115.9 us)
Async XLA Ops:
  8.0 427.1 %all-reduce.9.cloned.1.call-start = ((), (), s32[]{:S(2)}) async-start(), calls=%async_computation.1 | async-start | bytes 4718592 | tf_op jit(solution)/shard_map/psum | solution.py:656
  167.9 36.8 %collective-permute-start.8 = (bf16[512,1536]{1,0:T(8,128)(2,1)}, bf16[512,1536]{1,0:T(8,128)(2,1)}, u32[]{:S(2)}, u32[]{:S(2)}) collective-permute-start(bf16[512,1536]{1,0:T(8,128)(2,1)} %add_convert_fusion), channel_id=1, source_target_pairs={{0,2},{1,3},{2,0},{3,1},{4,6},{5,7},{6,4},{7,5},{8,10},{9,11},{10,... | collective-permute-start | bytes 4718600 | tf_op jit(solution)/shard_map/ppermute | solution.py:364
  177.9 297.2 %all-gather.2.cloned.1.call-start = ((), (), s32[]{:S(2)}) async-start(), calls=%async_computation | async-start | bytes 7864320 | tf_op jit(solution)/shard_map/all_gather | solution.py:725
  178.2 49.3 %collective-permute-start.3 = (bf16[1024,1536]{1,0:T(8,128)(2,1)}, bf16[1024,1536]{1,0:T(8,128)(2,1)}, u32[]{:S(2)}, u32[]{:S(2)}) collective-permute-start(bf16[1024,1536]{1,0:T(8,128)(2,1)} %get-tuple-element.44), channel_id=1, source_target_pairs={{0,1},{1,0},{2,3},{3,2},{4,5},{5,4},{6,7},{7,6},{8,9},{9,8},{10,11... | collective-permute-start | bytes 9437192 | tf_op jit(solution)/shard_map/ppermute | solution.py:364
  219.1 21.4 %collective-permute-start.9 = (bf16[864,256]{1,0:T(8,128)(2,1)S(1)}, bf16[864,256]{1,0:T(8,128)(2,1)S(1)}, u32[]{:S(2)}, u32[]{:S(2)}) collective-permute-start(bf16[864,256]{1,0:T(8,128)(2,1)S(1)} %fusion.12), channel_id=1, source_target_pairs={{0,1},{1,0},{2,3},{3,2},{4,5},{5,4},{6,7},{7,6},{8,9},{9,8},{10,11... | collective-permute-start | bytes 1327112 | tf_op jit(solution)/shard_map/ppermute | solution.py:364
  230.2 62.2 %collective-permute-start.4 = (bf16[512,1536]{1,0:T(8,128)(2,1)S(1)}, bf16[512,1536]{1,0:T(8,128)(2,1)S(1)}, u32[]{:S(2)}, u32[]{:S(2)}) collective-permute-start(bf16[512,1536]{1,0:T(8,128)(2,1)S(1)} %add_convert_fusion.2), channel_id=1, source_target_pairs={{0,2},{1,3},{2,0},{3,1},{4,6},{5,7},{6,4},{7,5},{8,10},{9,11},{10,... | collective-permute-start | bytes 4718600 | tf_op jit(solution)/shard_map/ppermute | solution.py:364
  237.4 63.5 %collective-permute-start.22 = (bf16[768,768]{1,0:T(8,128)(2,1)}, bf16[768,768]{1,0:T(8,128)(2,1)}, u32[]{:S(2)}, u32[]{:S(2)}) collective-permute-start(bf16[768,768]{1,0:T(8,128)(2,1)} %constant_dynamic-slice_fusion.1), channel_id=1, source_target_pairs={{0,4},{4,0},{8,12},{12,8},{16,20},{20,16},{24,28},{28,24},{1,5},{5... | collective-permute-start | bytes 3538952 | tf_op jit(solution)/shard_map/ppermute | solution.py:364
  240.0 64.5 %collective-permute-start.16 = (bf16[768,768]{1,0:T(8,128)(2,1)}, bf16[768,768]{1,0:T(8,128)(2,1)}, u32[]{:S(2)}, u32[]{:S(2)}) collective-permute-start(bf16[768,768]{1,0:T(8,128)(2,1)} %constant_dynamic-slice_fusion), channel_id=1, source_target_pairs={{0,4},{4,0},{8,12},{12,8},{16,20},{20,16},{24,28},{28,24},{1,5},{5... | collective-permute-start | bytes 3538952 | tf_op jit(solution)/shard_map/ppermute | solution.py:364
  240.9 57.6 %collective-permute-start.10 = (bf16[432,256]{1,0:T(8,128)(2,1)S(1)}, bf16[432,256]{1,0:T(8,128)(2,1)S(1)}, u32[]{:S(2)}, u32[]{:S(2)}) collective-permute-start(bf16[432,256]{1,0:T(8,128)(2,1)S(1)} %add_convert_fusion.10), channel_id=1, source_target_pairs={{0,2},{1,3},{2,0},{3,1},{4,6},{5,7},{6,4},{7,5},{8,10},{9,11},{10,... | collective-permute-start | bytes 663560 | tf_op jit(solution)/shard_map/ppermute | solution.py:364
  296.2 47.6 %collective-permute-start.5 = (bf16[512,1536]{1,0:T(8,128)(2,1)}, bf16[512,1536]{1,0:T(8,128)(2,1)}, u32[]{:S(2)}, u32[]{:S(2)}) collective-permute-start(bf16[512,1536]{1,0:T(8,128)(2,1)} %add_convert_fusion.1.value_ref), channel_id=1, source_target_pairs={{0,2},{1,3},{2,0},{3,1},{4,6},{5,7},{6,4},{7,5},{8,10},{9,11},{10,... | collective-permute-start | bytes 4718600 | tf_op jit(solution)/shard_map/ppermute | solution.py:364
  306.7 40.7 %collective-permute-start.17 = (bf16[384,768]{1,0:T(8,128)(2,1)}, bf16[384,768]{1,0:T(8,128)(2,1)}, u32[]{:S(2)}, u32[]{:S(2)}) collective-permute-start(bf16[384,768]{1,0:T(8,128)(2,1)} %add_convert_fusion.4), channel_id=1, source_target_pairs={{0,8},{4,12},{8,0},{12,4},{16,24},{20,28},{24,16},{28,20},{1,9},{5... | collective-permute-start | bytes 1769480 | tf_op jit(solution)/shard_map/ppermute | solution.py:364
  310.0 32.2 %collective-permute-start.12 = (bf16[92,1536]{1,0:T(8,128)(2,1)S(1)}, bf16[92,1536]{1,0:T(8,128)(2,1)S(1)}, u32[]{:S(2)}, u32[]{:S(2)}) collective-permute-start(bf16[92,1536]{1,0:T(8,128)(2,1)S(1)} %fusion.40), channel_id=1, source_target_pairs={{0,8},{4,12},{8,0},{12,4},{16,24},{20,28},{24,16},{28,20},{1,9},{5... | collective-permute-start | bytes 847880 | tf_op jit(solution)/shard_map/ppermute | solution.py:364
  320.7 47.5 %collective-permute-start.24 = (bf16[192,768]{1,0:T(8,128)(2,1)}, bf16[192,768]{1,0:T(8,128)(2,1)}, u32[]{:S(2)}, u32[]{:S(2)}) collective-permute-start(bf16[192,768]{1,0:T(8,128)(2,1)} %add_convert_fusion.6), channel_id=1, source_target_pairs={{0,16},{4,20},{8,24},{12,28},{16,0},{20,4},{24,8},{28,12},{1,17},{... | collective-permute-start | bytes 884744 | tf_op jit(solution)/shard_map/ppermute | solution.py:364
  342.3 21.9 %collective-permute-start.13 = (bf16[92,1536]{1,0:T(8,128)(2,1)S(1)}, bf16[92,1536]{1,0:T(8,128)(2,1)}, u32[]{:S(2)}, u32[]{:S(2)}) collective-permute-start(bf16[92,1536]{1,0:T(8,128)(2,1)S(1)} %add.313), channel_id=1, source_target_pairs={{0,16},{4,20},{8,24},{12,28},{16,0},{20,4},{24,8},{28,12},{1,17},{... | collective-permute-start | bytes 847880 | tf_op jit(solution)/shard_map/ppermute | solution.py:364
  347.4 122.8 %collective-permute-start.6 = (bf16[1024,1536]{1,0:T(8,128)(2,1)}, bf16[1024,1536]{1,0:T(8,128)(2,1)S(1)}, u32[]{:S(2)}, u32[]{:S(2)}) collective-permute-start(bf16[1024,1536]{1,0:T(8,128)(2,1)} %join.6.value_ref), channel_id=1, source_target_pairs={{0,1},{1,0},{2,3},{3,2},{4,5},{5,4},{6,7},{7,6},{8,9},{9,8},{10,11... | collective-permute-start | bytes 9437192 | tf_op jit(solution)/shard_map/ppermute | solution.py:364
  349.4 20.3 %collective-permute-start.18 = (bf16[192,768]{1,0:T(8,128)(2,1)}, bf16[192,768]{1,0:T(8,128)(2,1)}, u32[]{:S(2)}, u32[]{:S(2)}) collective-permute-start(bf16[192,768]{1,0:T(8,128)(2,1)} %add_convert_fusion.8), channel_id=1, source_target_pairs={{0,16},{4,20},{8,24},{12,28},{16,0},{20,4},{24,8},{28,12},{1,17},{... | collective-permute-start | bytes 884744 | tf_op jit(solution)/shard_map/ppermute | solution.py:364
  366.8 37.1 %collective-permute-start.14 = (bf16[432,256]{1,0:T(8,128)(2,1)}, bf16[432,256]{1,0:T(8,128)(2,1)}, u32[]{:S(2)}, u32[]{:S(2)}) collective-permute-start(bf16[432,256]{1,0:T(8,128)(2,1)} %reshape.226.value_ref), channel_id=1, source_target_pairs={{0,2},{1,3},{2,0},{3,1},{4,6},{5,7},{6,4},{7,5},{8,10},{9,11},{10,... | collective-permute-start | bytes 663560 | tf_op jit(solution)/shard_map/ppermute | solution.py:364
  369.6 21.2 %collective-permute-start.25 = (bf16[192,768]{1,0:T(8,128)(2,1)S(1)}, bf16[192,768]{1,0:T(8,128)(2,1)S(1)}, u32[]{:S(2)}, u32[]{:S(2)}) collective-permute-start(bf16[192,768]{1,0:T(8,128)(2,1)S(1)} %add_convert_fusion.5.value_ref), channel_id=1, source_target_pairs={{0,16},{4,20},{8,24},{12,28},{16,0},{20,4},{24,8},{28,12},{1,17},{... | collective-permute-start | bytes 884744 | tf_op jit(solution)/shard_map/ppermute | solution.py:364
  371.8 24.9 %collective-permute-start.19 = (bf16[192,768]{1,0:T(8,128)(2,1)}, bf16[192,768]{1,0:T(8,128)(2,1)}, u32[]{:S(2)}, u32[]{:S(2)}) collective-permute-start(bf16[192,768]{1,0:T(8,128)(2,1)} %add_convert_fusion.7.value_ref), channel_id=1, source_target_pairs={{0,16},{4,20},{8,24},{12,28},{16,0},{20,4},{24,8},{28,12},{1,17},{... | collective-permute-start | bytes 884744 | tf_op jit(solution)/shard_map/ppermute | solution.py:364
  393.4 16.5 %collective-permute-start.26 = (bf16[384,768]{1,0:T(8,128)(2,1)}, bf16[384,768]{1,0:T(8,128)(2,1)}, u32[]{:S(2)}, u32[]{:S(2)}) collective-permute-start(bf16[384,768]{1,0:T(8,128)(2,1)} %join.10.value_ref), channel_id=1, source_target_pairs={{0,8},{4,12},{8,0},{12,4},{16,24},{20,28},{24,16},{28,20},{1,9},{5... | collective-permute-start | bytes 1769480 | tf_op jit(solution)/shard_map/ppermute | solution.py:364
  398.8 23.1 %collective-permute-start.20 = (bf16[384,768]{1,0:T(8,128)(2,1)}, bf16[384,768]{1,0:T(8,128)(2,1)}, u32[]{:S(2)}, u32[]{:S(2)}) collective-permute-start(bf16[384,768]{1,0:T(8,128)(2,1)} %join.8.value_ref), channel_id=1, source_target_pairs={{0,8},{4,12},{8,0},{12,4},{16,24},{20,28},{24,16},{28,20},{1,9},{5... | collective-permute-start | bytes 1769480 | tf_op jit(solution)/shard_map/ppermute | solution.py:364
  405.8 22.1 %collective-permute-start.15 = (bf16[864,256]{1,0:T(8,128)(2,1)}, bf16[864,256]{1,0:T(8,128)(2,1)}, u32[]{:S(2)}, u32[]{:S(2)}) collective-permute-start(bf16[864,256]{1,0:T(8,128)(2,1)} %join.7.value_ref), channel_id=1, source_target_pairs={{0,1},{1,0},{2,3},{3,2},{4,5},{5,4},{6,7},{7,6},{8,9},{9,8},{10,11... | collective-permute-start | bytes 1327112 | tf_op jit(solution)/shard_map/ppermute | solution.py:364
  412.2 32.5 %collective-permute-start.27 = (bf16[768,768]{1,0:T(8,128)(2,1)}, bf16[768,768]{1,0:T(8,128)(2,1)}, u32[]{:S(2)}, u32[]{:S(2)}) collective-permute-start(bf16[768,768]{1,0:T(8,128)(2,1)} %join.11.value_ref), channel_id=1, source_target_pairs={{0,4},{4,0},{8,12},{12,8},{16,20},{20,16},{24,28},{28,24},{1,5},{5... | collective-permute-start | bytes 3538952 | tf_op jit(solution)/shard_map/ppermute | solution.py:364
  424.3 40.2 %collective-permute-start.21 = (bf16[768,768]{1,0:T(8,128)(2,1)}, bf16[768,768]{1,0:T(8,128)(2,1)}, u32[]{:S(2)}, u32[]{:S(2)}) collective-permute-start(bf16[768,768]{1,0:T(8,128)(2,1)} %join.9.value_ref), channel_id=1, source_target_pairs={{0,4},{4,0},{8,12},{12,8},{16,20},{20,16},{24,28},{28,24},{1,5},{5... | collective-permute-start | bytes 3538952 | tf_op jit(solution)/shard_map/ppermute | solution.py:364
  (26 other events, 345.3 us)
Sparse Core Ops, SparseCore 0:
  178.0 116.9 all-reduce.8
Sparse Core Ops, SparseCore 1:
  213.4 72.1 all-gather.1
where the time goes:
time: 498 us; the launch traced here: 489 us
  waiting for transfers between devices  174 us (35%)
  Pallas kernels  170 us (34%)
  other arithmetic  49.1 us (10%)
  matrix products  30.1 us (6%)
  starting transfers between devices  25.7 us (5%)
  local copies, waits for them, and re-layouts  23.6 us (5%)
  between operations  16.3 us (3%)
    ppermute x28, waiting for transfers between devices, swap(): return lax.ppermute(value, axis, [(i, i ^ bit) for i in range(size)])  174 us
    pallas_call x1, Pallas kernels, on_device(): pl.pallas_call(lead_kernel, grid=(tokens // lead,), in_specs=[by_rows(mod...  48.7 us
    pallas_call x1, Pallas kernels, on_device(): pl.pallas_call(backward_kernel, grid=(seqs, per_seq), in_specs=[at((T, wi...  47.2 us
    dot_general x5, matrix products, dot_tn(): lax.dot_general(a, b, (((0,), (0,)), ((), ())), preferred_element_type=f32)  30.1 us
    ppermute x28, starting transfers between devices, swap(): return lax.ppermute(value, axis, [(i, i ^ bit) for i in range(size)])  25.6 us
    pallas_call x1, Pallas kernels, on_device(): pl.pallas_call(group_kernel, grid_spec=pltpu.PrefetchScalarGridSpec(num_s...  20.6 us
    pallas_call x8, Pallas kernels, place(): pl.pallas_call(kernel, grid_spec=pltpu.PrefetchScalarGridSpec(num_scalar_...  20 us
    pallas_call x1, Pallas kernels, on_device(): pl.pallas_call(middle_kernel, grid_spec=pltpu.PrefetchScalarGridSpec(num_...  18.9 us
  transfers between devices with their start and end apart: 30, of which 16 were waited for; matrix products, arithmetic and copies ran while one was open for 17% of the time, Pallas kernels for 7%

commit v1 on v0

--- a/solution.py
+++ b/solution.py
@@ -2,7 +2,6 @@
 
 import jax
 import jax.numpy as jnp
-import numpy as np
 from jax import lax
 from jax.experimental import pallas as pl
 from jax.experimental.pallas import tpu as pltpu
@@ -63,12 +62,33 @@
     return lane_ref[0:1, :], -jnp.exp(lane_ref[1:2, :])
 
 
-def head_terms(z_ref, bias, rate, aux, tri_ref, e_ref, ex_ref):
+def ones_where(condition):
+    return jnp.where(condition, 1.0, 0.0).astype(bf16)
+
+
+def expansion(shape, head_width):
+    lane = lax.broadcasted_iota(jnp.int32, shape, 0)
+    owner = lax.broadcasted_iota(jnp.int32, shape, 1) // head_width
+    return ones_where((lane == owner) | (lane == owner + HALF))
+
+
+def reduction(shape, head_width):
+    owner = lax.broadcasted_iota(jnp.int32, shape, 0) // head_width
+    return ones_where(lax.broadcasted_iota(jnp.int32, shape, 1) == owner)
+
+
+def triangle():
+    row = lax.broadcasted_iota(jnp.int32, (T, T), 0)
+    col = lax.broadcasted_iota(jnp.int32, (T, T), 1)
+    return row, col
+
+
+def head_terms(z_ref, bias, rate, aux, tri, e_ref, ex_ref):
     z = z_ref[...] + bias
     tail = jnp.exp(-jnp.abs(z))
     step = jnp.maximum(z, 0.0) + jnp.log1p(tail)
     high, low = two_terms(step * rate)
-    cum = dot(tri_ref[...], high) + dot(tri_ref[...], low)
+    cum = dot(tri, high) + dot(tri, low)
     end = cum[T - 1 : T]
     dst = jnp.exp(cum) * aux[:, 3:4]
     dend = jnp.exp(end - cum) * aux[:, 4:5]
@@ -86,12 +106,16 @@
 
 def lead_kernel(
     tokens_ref, go_ref, aux_ref, pg_ref, gate_w, value_w, state_w, step_w, out_w,
-    vtaps_ref, staps_ref, vbias_ref, sbias_ref, heads_ref, skip_ref, ng_ref, e_ref, tri_ref,
+    vtaps_ref, staps_ref, vbias_ref, sbias_ref, heads_ref, skip_ref, ng_ref,
     normed_ref, gate_ref, vs_ref, z_ref, gno_ref, y_ref, act_ref, pre_ref, stat_ref, sin_ref,
-    ext_ref, state_ref, ex_ref, sum_ref, lane_ref,
+    ext_ref, state_ref, ex_ref, sum_ref, lane_ref, e_ref,
 ):
     rows, width = gate_ref.shape
     chunks = range(rows // T)
+
+    @pl.when(pl.program_id(0) == 0)
+    def _():
+        e_ref[...] = expansion(e_ref.shape, width // heads_ref.shape[1])
 
     @pl.when(pl.program_id(0) % (SEQ_LEN // rows) == 0)
     def _():
@@ -99,12 +123,17 @@
         ext_ref[0:8, :] = jnp.zeros_like(ext_ref[0:8, :])
 
     part = 32
-    for lo in range(0, rows, part):
-        hidden = tokens_ref[lo : lo + part, :].astype(f32)
+
+    def normalize(index, carry):
+        r = pl.ds(pl.multiple_of(index * part, part), part)
+        hidden = tokens_ref[r, :].astype(f32)
         inv = lax.rsqrt(jnp.mean(hidden * hidden, axis=1, keepdims=True) + eps_value)
         for k in range(pg_ref.shape[0]):
             c = slice(k * LANES, (k + 1) * LANES)
-            normed_ref[lo : lo + part, c] = (hidden[:, c] * inv * pg_ref[k : k + 1, :]).astype(bf16)
+            normed_ref[r, c] = (hidden[:, c] * inv * pg_ref[k : k + 1, :]).astype(bf16)
+        return carry
+
+    lax.fori_loop(0, rows // part, normalize, 0)
     z = dot_nt(normed_ref[...], step_w[...])
     z_ref[...] = jnp.zeros_like(z_ref)
     z_ref[:, : z.shape[1]] = z
@@ -114,9 +143,11 @@
     vs_ref[:, width:] = raw.astype(bf16)
     at = [pl.ds(k * T, T) for k in chunks]
     bias, rate = head_rows(heads_ref, lane_ref)
+    row, col = triangle()
+    tri = ones_where(row >= col)
     aux = [aux_ref[k].T for k in chunks]
     terms = [
-        head_terms(z_ref.at[at[k]], bias, rate, aux[k], tri_ref, e_ref, ex_ref.at[k])
+        head_terms(z_ref.at[at[k]], bias, rate, aux[k], tri, e_ref, ex_ref.at[k])
         for k in chunks
     ]
     keep = [
@@ -140,8 +171,6 @@
         act_ref[at[k], c] = act_bf
         return act, act_bf
 
-    row = lax.broadcasted_iota(jnp.int32, (T, T), 0)
-    col = lax.broadcasted_iota(jnp.int32, (T, T), 1)
     b_flip, c_mats, scores, fades = [], [], [], []
     for k in chunks:
         _, b_mat = activate(slice(width, width + N), k)
@@ -216,8 +245,8 @@
     def _():
         csum_ref[...] = jnp.zeros_like(csum_ref)
 
-    for chunk in range(stat_ref.shape[0]):
-        r = slice(chunk * T, (chunk + 1) * T)
+    def one(chunk, carry):
+        r = pl.ds(pl.multiple_of(chunk * T, T), T)
         scale = jnp.broadcast_to(stat_ref[chunk, 0:1, :], (LANES, T)).T
         slope_scale = jnp.broadcast_to(stat_ref[chunk, 1:2, :], (LANES, T)).T
         for pair in range(gate_ref.shape[1] // LANES):
@@ -238,36 +267,40 @@
             gate_grad_ref[r, c] = grad_gate.astype(bf16)
             csum_ref[8:16, c] += sum_rows(grad_mix * x)
             mix_ref[r, c] = grad_mix.astype(bf16)
-
+        return carry
+
+    lax.fori_loop(0, stat_ref.shape[0], one, 0)
     store_half(dot(normed_ref[...], out_w[...]).astype(bf16), sent_ref, kept_ref)
 
 
 def backward_kernel(
     mix_ref, y_ref, act_ref, pre_ref, vs_ref, z_ref, sin_ref, aux_ref,
-    vtaps_ref, staps_ref, heads_ref, skip_ref, e_ref, er_ref, tri_ref, triu_ref,
+    vtaps_ref, staps_ref, heads_ref, skip_ref,
     grad_ref, csum_ref,
-    back_ref, ext_ref, ex_ref, xd_ref, gd_ref, through_ref, lane_ref, part_ref,
+    back_ref, ext_ref, ex_ref, xd_ref, gd_ref, through_ref, lane_ref, part_ref, e_ref, er_ref,
 ):
     width = mix_ref.shape[1]
 
     @pl.when((pl.program_id(0) == 0) & (pl.program_id(1) == 0))
     def _():
         csum_ref[...] = jnp.zeros_like(csum_ref)
+        e_ref[...] = expansion(e_ref.shape, width // heads_ref.shape[1])
+        er_ref[...] = reduction(er_ref.shape, width // heads_ref.shape[1])
 
     @pl.when(pl.program_id(1) == 0)
     def _():
         back_ref[...] = jnp.zeros_like(back_ref)
         ext_ref[T : T + 8, :] = jnp.zeros_like(ext_ref[T : T + 8, :])
 
+    row, col = triangle()
+    tri, triu = ones_where(row >= col), ones_where(row <= col)
     bias, rate = head_rows(heads_ref, lane_ref)
     aux = aux_ref[0].T
-    z, step, cum, cum_t, carry = head_terms(z_ref, bias, rate, aux, tri_ref, e_ref, ex_ref)
+    z, step, cum, cum_t, carry = head_terms(z_ref, bias, rate, aux, tri, e_ref, ex_ref)
     keep = [jnp.broadcast_to(aux[:, 5 + s : 6 + s], (T, LANES)) for s in range(1, K)]
     b_mat = act_ref[:, width : width + N]
     c_mat = act_ref[:, width + N : width + 2 * N]
     scores_t = dot_nt(b_mat, c_mat)
-    row = lax.broadcasted_iota(jnp.int32, (T, T), 0)
-    col = lax.broadcasted_iota(jnp.int32, (T, T), 1)
     same = (aux[:, 5:6] == aux_ref[0, 5:6, :]) & (row <= col)
     fade = jnp.where(same, 0.0, NEG)
     lane = lax.broadcasted_iota(jnp.int32, (T, LANES), 1)
@@ -343,9 +376,9 @@
     by_head = [dot(part_ref[k], er_ref[...]) for k in range(5)]
     col_far, direct = by_head[3:]
     high, low = two_terms(by_head[0] + by_head[1] + by_head[2])
-    grad_acc = through_ref[0:1, :] + (dot(triu_ref[...], high) + dot(triu_ref[...], low))
+    grad_acc = through_ref[0:1, :] + (dot(triu, high) + dot(triu, low))
     high, low = two_terms(col_far)
-    grad_acc = grad_acc + (dot(tri_ref[...], high) + dot(tri_ref[...], low)) - col_far
+    grad_acc = grad_acc + (dot(tri, high) + dot(tri, low)) - col_far
     grad_step = direct + grad_acc * rate
     grad_z = grad_step * sigmoid(z)
     csum_ref[8 * (K + 1) : 8 * (K + 2), 0:LANES] += sum_rows(grad_z)
@@ -394,6 +427,21 @@
     )(jnp.reshape(slot, (1,)).astype(jnp.int32), value, *given)
 
 
+def copy_rows(value):
+    def kernel(value_ref, out_ref):
+        out_ref[...] = value_ref[...]
+
+    spec = pl.BlockSpec((block_of(value.shape[0]), value.shape[1]), lambda i: (i, 0))
+    return pl.pallas_call(
+        kernel,
+        grid=(value.shape[0] // spec.block_shape[0],),
+        in_specs=[spec],
+        out_specs=spec,
+        out_shape=jax.ShapeDtypeStruct(value.shape, value.dtype),
+        name="copy_rows",
+    )(value)
+
+
 def join(value, other, upper):
     rows, width = value.shape
     block = block_of(rows)
@@ -432,6 +480,54 @@
         piece = lax.dynamic_slice_in_dim(value, base + start, rows, 0).astype(f32)
         total = piece if total is None else total + piece
     return total
+
+
+def sum_quarters(kept, sent, arrays, rows, kernel):
+    index = lax.axis_index("tensor")
+    other = swap(sent, "tensor", 4, 1)
+    upper = index // 2
+    quarter, width = kept.shape[0] // 2, kept.shape[1]
+    out = add_parts([(kept, 0), (other, 0)], (1 - upper) * quarter, quarter).astype(kept.dtype)
+    last = swap(out, "tensor", 4, 2)
+    count = quarter // T
+    half = pl.BlockSpec((T, width), lambda i, s: (s[1] * count + i, 0))
+    own = pl.BlockSpec((T, width), lambda i, s: (s[0] * count + i, 0))
+    plain = pl.BlockSpec((T, width), lambda i, s: (i, 0))
+    return pl.pallas_call(
+        kernel,
+        grid_spec=pltpu.PrefetchScalarGridSpec(
+            num_scalar_prefetch=1,
+            grid=(count,),
+            in_specs=[half, half, plain]
+            + [own for _ in arrays]
+            + [pl.BlockSpec(v.shape, lambda i, s: (0, 0)) for v in rows],
+            out_specs=plain,
+        ),
+        out_shape=jax.ShapeDtypeStruct((quarter, width), bf16),
+        name="quarter",
+    )(jnp.stack([index, upper]).astype(jnp.int32), kept, other, last, *arrays, *rows)
+
+
+def block_kernel(_, kept_ref, other_ref, last_ref, tokens_ref, out_ref):
+    total = kept_ref[...].astype(f32) + other_ref[...].astype(f32) + last_ref[...].astype(f32)
+    out_ref[...] = (tokens_ref[...].astype(f32) + total).astype(bf16)
+
+
+def input_kernel(_, kept_ref, other_ref, last_ref, tokens_ref, grad_ref, gain_ref, out_ref):
+    part = 32
+
+    def one(index, carry):
+        r = pl.ds(pl.multiple_of(index * part, part), part)
+        total = kept_ref[r, :].astype(f32) + other_ref[r, :].astype(f32) + last_ref[r, :].astype(f32)
+        hidden = tokens_ref[r, :].astype(f32)
+        inv = lax.rsqrt(jnp.mean(hidden * hidden, axis=1, keepdims=True) + eps_value)
+        weighted = gain_ref[0:1, :] * total
+        mean = jnp.mean(weighted * hidden, axis=1, keepdims=True)
+        grad_hidden = inv * weighted - hidden * (inv * inv * inv * mean)
+        out_ref[r, :] = (grad_ref[r, :].astype(f32) + grad_hidden).astype(bf16)
+        return carry
+
+    lax.fori_loop(0, out_ref.shape[0] // part, one, 0)
 
 
 def scatter_halves(kept, sent, axis, size):
@@ -530,8 +626,9 @@
 
     model = in_ref.shape[1]
     part = model // 3 if model % 384 == 0 else model
-    for lo in range(0, model, part):
-        c = slice(lo, lo + part)
+
+    def one(index, carry):
+        c = pl.ds(pl.multiple_of(index * part, part), part)
         total, at = dot_nt(gate_ref[...], gate_w[c, :]) + dot(steps, step_w[:, c]), 0
         for w in weights:
             total = total + dot_nt(packed_ref[:, at : at + w.shape[1]], w[c, :])
@@ -539,6 +636,9 @@
         rounded = total.astype(bf16)
         in_ref[:, c] = rounded
         gain_ref[:, c] += sum_rows(rounded.astype(f32) * normed_ref[:, c].astype(f32))
+        return carry
+
+    lax.fori_loop(0, model // part, one, 0)
     store_half(in_ref[...], sent_ref, kept_ref)
 
 
@@ -574,24 +674,10 @@
     decay_rate = -jnp.exp(decay_log)
     skip = jnp.repeat(skip_gain, head_width).reshape(width // LANES, LANES)
     gain = norm_gain.reshape(width // LANES, LANES)
-    lanes = np.arange(LANES)
-    owner = np.arange(width) // head_width
-    expand = jnp.asarray(lanes[:, None] % HALF == owner[None, :], bf16)
-    reduce = jnp.asarray(owner[:, None] == lanes[None, :], bf16)
-    rows = np.arange(T)
-    tri = jnp.asarray(rows[:, None] >= rows[None, :], bf16)
-    triu = jnp.asarray(rows[:, None] <= rows[None, :], bf16)
-
-    def at(block, index):
-        return pl.BlockSpec(block, index)
-
-    def whole(value):
-        return pl.BlockSpec(value.shape, lambda i, j: (0,) * value.ndim, pipeline_mode=pl.Buffered(1))
-
     sds = jax.ShapeDtypeStruct
     pg_rows = pre_gain.reshape(model // LANES, LANES)
     consts = (pg_rows,) + projections + (out_proj, conv_value, conv_state, vbias, sbias)
-    consts += (head_pair, skip, gain, expand, tri)
+    consts += (head_pair, skip, gain)
     normed, gate_raw, vs_raw, z_raw, grad_normed_out, y, act, pre, stat, sin = pl.pallas_call(
         lead_kernel,
         grid=(tokens // lead,),
@@ -608,7 +694,7 @@
         scratch_shapes=[
             pltpu.VMEM((lead + 8, wide), f32), pltpu.VMEM((N, width), f32),
             pltpu.VMEM((lead // T, 3 * T, width), f32), pltpu.VMEM((lead // T, 2, T, LANES), f32),
-            pltpu.VMEM((8, LANES), f32),
+            pltpu.VMEM((8, LANES), f32), pltpu.VMEM((LANES, width), bf16),
         ],
         name="lead",
     )(tokens_in, grad_out, aux, *consts)
@@ -659,41 +745,47 @@
 
     start = lax.axis_index("tensor") * (tokens // n_tensor)
     own = lambda v: lax.dynamic_slice_in_dim(v, start, tokens // n_tensor, 0)
-    branch = scatter_halves(kept, sent, "tensor", n_tensor)
-    own_hidden = own(tokens_in).astype(f32)
-    block_out = (own_hidden + branch).astype(bf16)
     if n_tensor == 4:
+        block_out = sum_quarters(kept, sent, (tokens_in,), (), block_kernel)
         block_out = gather_rows(block_out, "tensor", n_tensor, bf16, mixed=True)
     else:
+        branch = scatter_halves(kept, sent, "tensor", n_tensor)
+        block_out = (own(tokens_in).astype(f32) + branch).astype(bf16)
         block_out = lax.all_gather(block_out, "tensor", axis=0, tiled=True)
 
-    consts = (conv_value, conv_state, head_pair, skip, expand, reduce, tri, triu)
-    bwd = lambda i, j: (i * per_seq + per_seq - 1 - j, 0)
-    bwd3 = lambda i, j: (i * per_seq + per_seq - 1 - j, 0, 0)
+    consts = (conv_value, conv_state, head_pair, skip)
+    given = (mix, y, act, pre, vs_raw, z_raw, sin, aux)
+    out = [sds((tokens, full), bf16), sds((8 * (K + 2), wide), f32)]
+
+    def of(value):
+        row = lambda i, j: i * per_seq + per_seq - 1 - j
+        if len(value.shape) == 2:
+            return pl.BlockSpec((T, value.shape[1]), lambda i, j: (row(i, j), 0))
+        return pl.BlockSpec((1,) + value.shape[1:], lambda i, j: (row(i, j), 0, 0))
+
+    def whole(value):
+        return pl.BlockSpec(value.shape, lambda i, j: (0, 0), pipeline_mode=pl.Buffered(1))
+
     packed, csum = pl.pallas_call(
         backward_kernel,
         grid=(seqs, per_seq),
-        in_specs=[
-            at((T, width), bwd), at((T, width), bwd), at((T, wide), bwd), at((T, wide), bwd),
-            at((T, wide), bwd), at((T, LANES), bwd), at((1, N, width), bwd3),
-            at((1, 16, T), bwd3),
-        ] + [whole(v) for v in consts],
-        out_specs=[
-            at((T, full), bwd), pl.BlockSpec((8 * (K + 2), wide), lambda i, j: (0, 0)),
-        ],
-        out_shape=[sds((tokens, full), bf16), sds((8 * (K + 2), wide), f32)],
+        in_specs=[of(v) for v in given] + [whole(v) for v in consts],
+        out_specs=[of(out[0]), pl.BlockSpec(out[1].shape, lambda i, j: (0, 0))],
+        out_shape=out,
         scratch_shapes=[
             pltpu.VMEM((N, width), f32), pltpu.VMEM((T + 8, wide), f32),
             pltpu.VMEM((3 * T, width), f32), pltpu.VMEM((T, width), bf16),
             pltpu.VMEM((T, width), bf16), pltpu.VMEM((8, LANES), f32),
             pltpu.VMEM((8, LANES), f32), pltpu.VMEM((5, T, width), bf16),
+            pltpu.VMEM((LANES, width), bf16), pltpu.VMEM((width, LANES), bf16),
         ],
         name="ssd_backward",
-    )(mix, y, act, pre, vs_raw, z_raw, sin, aux, *consts)
-
-    grad_value_proj = dot_tn(normed, packed[:, :width]).astype(bf16)
-    grad_state_proj = dot_tn(normed, packed[:, width:wide]).astype(bf16)
-    grad_step_proj = dot_tn(packed[:, wide:], normed)[:heads]
+    )(*given, *consts)
+
+    grad_packed = dot_tn(normed, packed).astype(bf16)
+    grad_value_proj = grad_packed[:, :width]
+    grad_state_proj = grad_packed[:, width:wide]
+    grad_step_proj = grad_packed[:, wide : wide + heads].T
     sent, kept, gain_part = pl.pallas_call(
         group_kernel,
         grid_spec=pltpu.PrefetchScalarGridSpec(
@@ -713,16 +805,20 @@
 
     grad_value_proj = reduce_rows(grad_value_proj, "dp", n_dp, f32)
 
-    grad_normed = scatter_halves(kept, sent, "tensor", n_tensor)
-    tokens_late, _ = lax.optimization_barrier((tokens_in, kept))
-    own_hidden = own(tokens_late).astype(f32)
-    own_inv = lax.rsqrt(jnp.mean(own_hidden * own_hidden, axis=1, keepdims=True) + eps_value)
-    weighted = pre_gain * grad_normed
-    grad_hidden = own_inv * weighted - own_hidden * (own_inv * own_inv * own_inv) * jnp.mean(
-        weighted * own_hidden, axis=1, keepdims=True
-    )
-    grad_in = (own(grad_out).astype(f32) + grad_hidden).astype(bf16)
+    if n_tensor == 4:
+        gain_row = pre_gain[None, :]
+        grad_in = sum_quarters(kept, sent, (tokens_in, grad_out), (gain_row,), input_kernel)
+    else:
+        grad_normed = scatter_halves(kept, sent, "tensor", n_tensor)
+        own_hidden = own(tokens_in).astype(f32)
+        own_inv = lax.rsqrt(jnp.mean(own_hidden * own_hidden, axis=1, keepdims=True) + eps_value)
+        weighted = pre_gain * grad_normed
+        grad_hidden = own_inv * weighted - own_hidden * (own_inv * own_inv * own_inv) * jnp.mean(
+            weighted * own_hidden, axis=1, keepdims=True
+        )
+        grad_in = (own(grad_out).astype(f32) + grad_hidden).astype(bf16)
     grad_in = lax.all_gather(grad_in, "tensor", axis=0, tiled=True)
+    grad_in = copy_rows(grad_in)
 
     gain_rows = model // (2 * N)
     extra = jnp.concatenate([sums[:, width:], gain_part.reshape(gain_rows, 2 * N)], axis=0)

time: 498 us -> 500 us (level); the launches traced: 489 us -> 499 us
  Pallas kernels: 170 us -> 195 us
  other arithmetic: 49.1 us -> 36.8 us
    pallas_call x1 -> x4, Pallas kernels: 47.2 us -> 65.1 us  [the longest x1 47 us: on_device(): pl.pallas_call(backward_kernel, grid=(seqs, per_seq), in_specs=[of(v) for...]
    convert_element_type x7 -> x5, other arithmetic: 14.8 us -> 7.59 us  [scatter_parts(): sent = add_parts(parts, (1 - upper) * rows, rows).astype(value.dtype)]
    pallas_call x1, Pallas kernels: 48.7 us -> 55 us  [on_device(): pl.pallas_call(lead_kernel, grid=(tokens // lead,), in_specs=[by_rows(mod...]
    dot_general x5 -> x3, matrix products: 30.1 us -> 27.2 us  [dot_tn(): lax.dot_general(a, b, (((0,), (0,)), ((), ())), preferred_element_type=f32)]
  transfers between devices with their start and end apart: 30 -> 30, of which waited for: 16 -> 14; matrix products, arithmetic and copies ran while one was open for 17% -> 14% of each run, Pallas kernels for 7% -> 9%
where the time goes in v1:
time: 500 us; the launch traced here: 499 us
  Pallas kernels  195 us (39%)
  waiting for transfers between devices  175 us (35%)
  other arithmetic  36.8 us (7%)
  starting transfers between devices  29.1 us (6%)
  matrix products  27.2 us (5%)
  local copies, waits for them, and re-layouts  20.3 us (4%)
  between operations  15.9 us (3%)
    ppermute x28, waiting for transfers between devices, swap(): return lax.ppermute(value, axis, [(i, i ^ bit) for i in range(size)])  175 us
    pallas_call x1, Pallas kernels, on_device(): pl.pallas_call(lead_kernel, grid=(tokens // lead,), in_specs=[by_rows(mod...  55 us
    pallas_call x1, Pallas kernels, on_device(): pl.pallas_call(backward_kernel, grid=(seqs, per_seq), in_specs=[of(v) for...  47 us
    ppermute x28, starting transfers between devices, swap(): return lax.ppermute(value, axis, [(i, i ^ bit) for i in range(size)])  29 us
    dot_general x3, matrix products, dot_tn(): lax.dot_general(a, b, (((0,), (0,)), ((), ())), preferred_element_type=f32)  27.2 us
    pallas_call x1, Pallas kernels, on_device(): pl.pallas_call(group_kernel, grid_spec=pltpu.PrefetchScalarGridSpec(num_s...  21.6 us
    pallas_call x8, Pallas kernels, place(): pl.pallas_call(kernel, grid_spec=pltpu.PrefetchScalarGridSpec(num_scalar_...  20 us
    pallas_call x1, Pallas kernels, on_device(): pl.pallas_call(middle_kernel, grid_spec=pltpu.PrefetchScalarGridSpec(num_...  19.4 us
  transfers between devices with their start and end apart: 30, of which 14 were waited for; matrix products, arithmetic and copies ran while one was open for 14% of the time, Pallas kernels for 9%

profile of v1, /device:TPU:0, one launch (start us, length us, event | category | flops | bytes accessed | tf_op | source)
XLA Modules:
  0.0 498.7 jit_solution(6256557382701515763)
XLA Ops:
  14.6 55.0 %lead.1 = (bf16[2048,1536]{1,0:T(8,128)(2,1)}, bf16[2048,768]{1,0:T(8,128)(2,1)}, bf16[2048,1024]{1,0:T(8,128)(2,1)}, f32[2048,128]{1,0:T(8,128)}, bf16[2048,768...) custom-call(bf16[2048,1536]{1,0:T(8,128)(2,1)} %tokens_ref.5, ...), custom_call_target="tpu_custom_call" | custom-call | tf_op jit(solution)/shard_map/lead/pallas_call | solution.py:681
  77.4 19.4 %middle.1 = (bf16[2048,768]{1,0:T(8,128)(2,1)}, bf16[2048,768]{1,0:T(8,128)(2,1)}, bf16[2048,768]{1,0:T(8,128)(2,1)}, bf16[1024,1536]{1,0:T(8,128)(2,1)}, bf16[1024,1536]{1,0:T(8,128)(2,1)}, /*index=5*/f32[16,768]{1,0:T(8,128)}) custom-call(s32[1]{0:T(128)} %bitcast.4._.slot_ref, bf16[2048,768]{1,0:T(8,128)(2,1)} %get-tuple-element.37.gate_ref, ...), custom_call_target="tpu_custom_call" | custom-call | tf_op jit(solution)/shard_map/middle/pallas_call | solution.py:726
  96.7 47.0 %ssd_backward.1 = (bf16[2048,1152]{1,0:T(8,128)(2,1)}, f32[48,1024]{1,0:T(8,128)}) custom-call(bf16[2048,768]{1,0:T(8,128)(2,1)} %get-tuple-element.45.mix_ref, f32[2048,768]{1,0:T(8,128)} %get-tuple-element.39.y_ref, bf16[2048,1024]{1,0:T(8,128)(2,1)} %get-tuple-element.40.act_ref, bf16[2048,1024]{1,0:T(8,128)(2,1)} %get-tuple-element.46.pre_ref, ...), custom_call_target="tpu_custom_call" | custom-call | tf_op jit(solution)/shard_map/ssd_backward/pallas_call | solution.py:769
  143.7 21.6 %group_in.1 = (bf16[1024,1536]{1,0:T(8,128)(2,1)}, bf16[1024,1536]{1,0:T(8,128)(2,1)}, f32[8,1536]{1,0:T(8,128)}) custom-call(s32[1]{0:T(128)} %bitcast.4._.slot_ref, bf16[2048,768]{1,0:T(8,128)(2,1)} %get-tuple-element.44.gate_ref, bf16[2048,1152]{1,0:T(8,128)(2,1)} %get-tuple-element.50.packed_ref, bf16[2048,1536]{1,0:T(8,128)(2,1)} %get-tuple-element.51.normed_ref, ...), custom_call_target="tpu_custom_call" | custom-call | tf_op jit(solution)/shard_map/group_in/pallas_call | solution.py:789
  165.4 9.5 %convolution_convert_fusion.1 = bf16[768,1536]{1,0:T(8,128)(2,1)} fusion(bf16[2048,768]{1,0:T(8,128)(2,1)} %get-tuple-element.57, bf16[2048,1536]{1,0:T(8,128)(2,1)} %grad_ref.1), kind=kOutput, calls=%fused_computation.1 | convolution fusion | flops 4833017856 | bytes 11796480 | tf_op jit(solution)/shard_map/dot_general | solution.py:32
  179.8 35.0 %collective-permute-done.8.last_ref = bf16[512,1536]{1,0:T(8,128)(2,1)S(1)} collective-permute-done((bf16[512,1536]{1,0:T(8,128)(2,1)}, bf16[512,1536]{1,0:T(8,128)(2,1)S(1)}, u32[]{:S(2)}, u32[]{:S(2)}) %collective-permute-start.8) | collective-permute-done | bytes 1572896 | tf_op jit(solution)/shard_map/ppermute | solution.py:397
  215.9 6.8 %quarter.3 = bf16[512,1536]{1,0:T(8,128)(2,1)} custom-call(s32[2]{0:T(128)} %pad_add_fusion._, bf16[1024,1536]{1,0:T(8,128)(2,1)} %get-tuple-element.52.kept_ref, bf16[1024,1536]{1,0:T(8,128)(2,1)} %collective-permute-done.7.other_ref, bf16[512,1536]{1,0:T(8,128)(2,1)} %copy-done.6, bf16[2048,1536]{1,0:T(8,128)(2,1)} %tokens_ref.5, ...), custom_call_target="tpu_custom_call" | custom-call | tf_op jit(solution)/shard_map/quarter/pallas_call | solution.py:496
  222.9 12.1 %convolution_convert_fusion = bf16[1536,1152]{1,0:T(8,128)(2,1)S(1)} fusion(bf16[2048,1536]{1,0:T(8,128)(2,1)} %get-tuple-element.51.normed_ref, bf16[2048,1152]{1,0:T(8,128)(2,1)} %get-tuple-element.50.packed_ref), kind=kOutput, calls=%fused_computation | convolution fusion | flops 7249526784 | bytes 14548992 | tf_op jit(solution)/shard_map/dot_general | solution.py:32
  236.0 3.3 add_convert_fusion.1
  240.0 5.5 %convolution_convert_fusion.2 = bf16[1536,768]{1,0:T(8,128)(2,1)S(1)} fusion(bf16[2048,1536]{1,0:T(8,128)(2,1)S(1)} %bitcast.57, bf16[2048,768]{1,0:T(8,128)(2,1)S(1)} %copy-done.3), kind=kOutput, calls=%fused_computation.2 | convolution fusion | flops 4833017856 | bytes 11796480 | tf_op jit(solution)/shard_map/dot_general | solution.py:32
  252.5 49.6 %collective-permute-done.4.last_ref = bf16[512,1536]{1,0:T(8,128)(2,1)} collective-permute-done((bf16[512,1536]{1,0:T(8,128)(2,1)S(1)}, bf16[512,1536]{1,0:T(8,128)(2,1)}, u32[]{:S(2)}, u32[]{:S(2)}) %collective-permute-start.4) | collective-permute-done | bytes 1572896 | tf_op jit(solution)/shard_map/ppermute | solution.py:397
  302.1 5.4 %quarter.2.value_ref = bf16[512,1536]{1,0:T(8,128)(2,1)} custom-call(s32[2]{0:T(128)} %pad_add_fusion._, bf16[1024,1536]{1,0:T(8,128)(2,1)} %get-tuple-element.42.kept_ref, bf16[1024,1536]{1,0:T(8,128)(2,1)} %collective-permute-done.3.other_ref, bf16[512,1536]{1,0:T(8,128)(2,1)} %collective-permute-done.4.last_ref, bf16[2048,1536]{1,0:T(8,128)(2,1)} %tokens_ref.5), custom_call_target="tpu_custom_call" | custom-call | tf_op jit(solution)/shard_map/quarter/pallas_call | solution.py:496
  322.7 9.5 %collective-permute-done.23 = bf16[384,768]{1,0:T(8,128)(2,1)} collective-permute-done((bf16[384,768]{1,0:T(8,128)(2,1)}, bf16[384,768]{1,0:T(8,128)(2,1)}, u32[]{:S(2)}, u32[]{:S(2)}) %collective-permute-start.23) | collective-permute-done | bytes 589856 | tf_op jit(solution)/shard_map/ppermute | solution.py:397
  336.5 18.7 %collective-permute-done.12 = bf16[92,1536]{1,0:T(8,128)(2,1)} collective-permute-done((bf16[92,1536]{1,0:T(8,128)(2,1)S(1)}, bf16[92,1536]{1,0:T(8,128)(2,1)}, u32[]{:S(2)}, u32[]{:S(2)}) %collective-permute-start.12) | collective-permute-done | bytes 282656 | tf_op jit(solution)/shard_map/ppermute | solution.py:397
  357.5 3.6 join.6.value_ref
  364.2 13.2 %collective-permute-done.13 = bf16[92,1536]{1,0:T(8,128)(2,1)} collective-permute-done((bf16[92,1536]{1,0:T(8,128)(2,1)S(1)}, bf16[92,1536]{1,0:T(8,128)(2,1)}, u32[]{:S(2)}, u32[]{:S(2)}) %collective-permute-start.13) | collective-permute-done | bytes 282656 | tf_op jit(solution)/shard_map/ppermute | solution.py:397
  386.1 10.3 %collective-permute-done.25.other_ref = bf16[192,768]{1,0:T(8,128)(2,1)S(1)} collective-permute-done((bf16[192,768]{1,0:T(8,128)(2,1)S(1)}, bf16[192,768]{1,0:T(8,128)(2,1)S(1)}, u32[]{:S(2)}, u32[]{:S(2)}) %collective-permute-start.25) | collective-permute-done | bytes 294944 | tf_op jit(solution)/shard_map/ppermute | solution.py:397
  399.0 4.8 collective-permute-start.26
  403.8 5.0 collective-permute-done.19.other_ref
  416.3 4.1 collective-permute-done.26.other_ref
  424.1 8.2 %collective-permute-done.20.other_ref = bf16[384,768]{1,0:T(8,128)(2,1)S(1)} collective-permute-done((bf16[384,768]{1,0:T(8,128)(2,1)}, bf16[384,768]{1,0:T(8,128)(2,1)S(1)}, u32[]{:S(2)}, u32[]{:S(2)}) %collective-permute-start.20) | collective-permute-done | bytes 589856 | tf_op jit(solution)/shard_map/ppermute | solution.py:397
  446.3 4.5 convert_element_type.240
  459.5 16.0 %collective-permute-done.21.value_ref = bf16[768,768]{1,0:T(8,128)(2,1)S(1)} collective-permute-done((bf16[768,768]{1,0:T(8,128)(2,1)}, bf16[768,768]{1,0:T(8,128)(2,1)S(1)}, u32[]{:S(2)}, u32[]{:S(2)}) %collective-permute-start.21) | collective-permute-done | bytes 1179680 | tf_op jit(solution)/shard_map/ppermute | solution.py:397
  485.4 5.9 %copy_rows.1 = bf16[2048,1536]{1,0:T(8,128)(2,1)} custom-call(bf16[2048,1536]{1,0:T(8,128)(2,1)} %all-gather.2.cloned.1.call-done.value_ref), custom_call_target="tpu_custom_call" | custom-call | tf_op jit(solution)/shard_map/copy_rows/pallas_call | solution.py:435
  (183 shorter events, 109.0 us)
Async XLA Ops:
  8.0 438.3 %all-reduce.9.cloned.1.call-start = ((), (), s32[]{:S(2)}) async-start(), calls=%async_computation.1 | async-start | bytes 4718592 | tf_op jit(solution)/shard_map/psum | solution.py:742
  174.9 310.4 %all-gather.2.cloned.1.call-start = ((), (), s32[]{:S(2)}) async-start(), calls=%async_computation | async-start | bytes 7864320 | tf_op jit(solution)/shard_map/all_gather | solution.py:820
  178.0 36.8 %collective-permute-start.8 = (bf16[512,1536]{1,0:T(8,128)(2,1)}, bf16[512,1536]{1,0:T(8,128)(2,1)S(1)}, u32[]{:S(2)}, u32[]{:S(2)}) collective-permute-start(bf16[512,1536]{1,0:T(8,128)(2,1)} %add_convert_fusion), channel_id=1, source_target_pairs={{0,2},{1,3},{2,0},{3,1},{4,6},{5,7},{6,4},{7,5},{8,10},{9,11},{10,... | collective-permute-start | bytes 4718600 | tf_op jit(solution)/shard_map/ppermute | solution.py:397
  178.6 57.4 %collective-permute-start.3 = (bf16[1024,1536]{1,0:T(8,128)(2,1)}, bf16[1024,1536]{1,0:T(8,128)(2,1)}, u32[]{:S(2)}, u32[]{:S(2)}) collective-permute-start(bf16[1024,1536]{1,0:T(8,128)(2,1)} %get-tuple-element.43), channel_id=1, source_target_pairs={{0,1},{1,0},{2,3},{3,2},{4,5},{5,4},{6,7},{7,6},{8,9},{9,8},{10,11... | collective-permute-start | bytes 9437192 | tf_op jit(solution)/shard_map/ppermute | solution.py:397
  239.2 62.8 %collective-permute-start.4 = (bf16[512,1536]{1,0:T(8,128)(2,1)S(1)}, bf16[512,1536]{1,0:T(8,128)(2,1)}, u32[]{:S(2)}, u32[]{:S(2)}) collective-permute-start(bf16[512,1536]{1,0:T(8,128)(2,1)S(1)} %add_convert_fusion.1), channel_id=1, source_target_pairs={{0,2},{1,3},{2,0},{3,1},{4,6},{5,7},{6,4},{7,5},{8,10},{9,11},{10,... | collective-permute-start | bytes 4718600 | tf_op jit(solution)/shard_map/ppermute | solution.py:397
  247.0 66.7 %collective-permute-start.22 = (bf16[768,768]{1,0:T(8,128)(2,1)}, bf16[768,768]{1,0:T(8,128)(2,1)}, u32[]{:S(2)}, u32[]{:S(2)}) collective-permute-start(bf16[768,768]{1,0:T(8,128)(2,1)} %constant_dynamic-slice_fusion.1), channel_id=1, source_target_pairs={{0,4},{4,0},{8,12},{12,8},{16,20},{20,16},{24,28},{28,24},{1,5},{5... | collective-permute-start | bytes 3538952 | tf_op jit(solution)/shard_map/ppermute | solution.py:397
  249.7 67.5 %collective-permute-start.16 = (bf16[768,768]{1,0:T(8,128)(2,1)}, bf16[768,768]{1,0:T(8,128)(2,1)}, u32[]{:S(2)}, u32[]{:S(2)}) collective-permute-start(bf16[768,768]{1,0:T(8,128)(2,1)} %constant_dynamic-slice_fusion), channel_id=1, source_target_pairs={{0,4},{4,0},{8,12},{12,8},{16,20},{20,16},{24,28},{28,24},{1,5},{5... | collective-permute-start | bytes 3538952 | tf_op jit(solution)/shard_map/ppermute | solution.py:397
  251.2 58.5 %collective-permute-start.10 = (bf16[432,256]{1,0:T(8,128)(2,1)}, bf16[432,256]{1,0:T(8,128)(2,1)}, u32[]{:S(2)}, u32[]{:S(2)}) collective-permute-start(bf16[432,256]{1,0:T(8,128)(2,1)} %add_convert_fusion.9), channel_id=1, source_target_pairs={{0,2},{1,3},{2,0},{3,1},{4,6},{5,7},{6,4},{7,5},{8,10},{9,11},{10,... | collective-permute-start | bytes 663560 | tf_op jit(solution)/shard_map/ppermute | solution.py:397
  307.5 50.1 %collective-permute-start.5 = (bf16[512,1536]{1,0:T(8,128)(2,1)}, bf16[512,1536]{1,0:T(8,128)(2,1)}, u32[]{:S(2)}, u32[]{:S(2)}) collective-permute-start(bf16[512,1536]{1,0:T(8,128)(2,1)} %quarter.2.value_ref), channel_id=1, source_target_pairs={{0,2},{1,3},{2,0},{3,1},{4,6},{5,7},{6,4},{7,5},{8,10},{9,11},{10,... | collective-permute-start | bytes 4718600 | tf_op jit(solution)/shard_map/ppermute | solution.py:397
  315.7 16.5 %collective-permute-start.23 = (bf16[384,768]{1,0:T(8,128)(2,1)}, bf16[384,768]{1,0:T(8,128)(2,1)}, u32[]{:S(2)}, u32[]{:S(2)}) collective-permute-start(bf16[384,768]{1,0:T(8,128)(2,1)} %add_convert_fusion.2), channel_id=1, source_target_pairs={{0,8},{4,12},{8,0},{12,4},{16,24},{20,28},{24,16},{28,20},{1,9},{5... | collective-permute-start | bytes 1769480 | tf_op jit(solution)/shard_map/ppermute | solution.py:397
  318.5 42.7 %collective-permute-start.17 = (bf16[384,768]{1,0:T(8,128)(2,1)S(1)}, bf16[384,768]{1,0:T(8,128)(2,1)}, u32[]{:S(2)}, u32[]{:S(2)}) collective-permute-start(bf16[384,768]{1,0:T(8,128)(2,1)S(1)} %add_convert_fusion.3), channel_id=1, source_target_pairs={{0,8},{4,12},{8,0},{12,4},{16,24},{20,28},{24,16},{28,20},{1,9},{5... | collective-permute-start | bytes 1769480 | tf_op jit(solution)/shard_map/ppermute | solution.py:397
  321.0 34.2 %collective-permute-start.12 = (bf16[92,1536]{1,0:T(8,128)(2,1)S(1)}, bf16[92,1536]{1,0:T(8,128)(2,1)}, u32[]{:S(2)}, u32[]{:S(2)}) collective-permute-start(bf16[92,1536]{1,0:T(8,128)(2,1)S(1)} %fusion.30), channel_id=1, source_target_pairs={{0,8},{4,12},{8,0},{12,4},{16,24},{20,28},{24,16},{28,20},{1,9},{5... | collective-permute-start | bytes 847880 | tf_op jit(solution)/shard_map/ppermute | solution.py:397
  334.1 46.2 %collective-permute-start.24 = (bf16[192,768]{1,0:T(8,128)(2,1)}, bf16[192,768]{1,0:T(8,128)(2,1)}, u32[]{:S(2)}, u32[]{:S(2)}) collective-permute-start(bf16[192,768]{1,0:T(8,128)(2,1)} %add_convert_fusion.5), channel_id=1, source_target_pairs={{0,16},{4,20},{8,24},{12,28},{16,0},{20,4},{24,8},{28,12},{1,17},{... | collective-permute-start | bytes 884744 | tf_op jit(solution)/shard_map/ppermute | solution.py:397
  356.2 21.2 %collective-permute-start.13 = (bf16[92,1536]{1,0:T(8,128)(2,1)S(1)}, bf16[92,1536]{1,0:T(8,128)(2,1)}, u32[]{:S(2)}, u32[]{:S(2)}) collective-permute-start(bf16[92,1536]{1,0:T(8,128)(2,1)S(1)} %add.258), channel_id=1, source_target_pairs={{0,16},{4,20},{8,24},{12,28},{16,0},{20,4},{24,8},{28,12},{1,17},{... | collective-permute-start | bytes 847880 | tf_op jit(solution)/shard_map/ppermute | solution.py:397
  361.2 121.0 %collective-permute-start.6 = (bf16[1024,1536]{1,0:T(8,128)(2,1)}, bf16[1024,1536]{1,0:T(8,128)(2,1)}, u32[]{:S(2)}, u32[]{:S(2)}) collective-permute-start(bf16[1024,1536]{1,0:T(8,128)(2,1)} %join.6.value_ref), channel_id=1, source_target_pairs={{0,1},{1,0},{2,3},{3,2},{4,5},{5,4},{6,7},{7,6},{8,9},{9,8},{10,11... | collective-permute-start | bytes 9437192 | tf_op jit(solution)/shard_map/ppermute | solution.py:397
  362.5 20.4 %collective-permute-start.18 = (bf16[192,768]{1,0:T(8,128)(2,1)S(1)}, bf16[192,768]{1,0:T(8,128)(2,1)}, u32[]{:S(2)}, u32[]{:S(2)}) collective-permute-start(bf16[192,768]{1,0:T(8,128)(2,1)S(1)} %add_convert_fusion.7), channel_id=1, source_target_pairs={{0,16},{4,20},{8,24},{12,28},{16,0},{20,4},{24,8},{28,12},{1,17},{... | collective-permute-start | bytes 884744 | tf_op jit(solution)/shard_map/ppermute | solution.py:397
  378.6 35.3 %collective-permute-start.14 = (bf16[432,256]{1,0:T(8,128)(2,1)S(1)}, bf16[432,256]{1,0:T(8,128)(2,1)}, u32[]{:S(2)}, u32[]{:S(2)}) collective-permute-start(bf16[432,256]{1,0:T(8,128)(2,1)S(1)} %reshape.207.value_ref), channel_id=1, source_target_pairs={{0,2},{1,3},{2,0},{3,1},{4,6},{5,7},{6,4},{7,5},{8,10},{9,11},{10,... | collective-permute-start | bytes 663560 | tf_op jit(solution)/shard_map/ppermute | solution.py:397
  381.6 14.8 %collective-permute-start.25 = (bf16[192,768]{1,0:T(8,128)(2,1)S(1)}, bf16[192,768]{1,0:T(8,128)(2,1)S(1)}, u32[]{:S(2)}, u32[]{:S(2)}) collective-permute-start(bf16[192,768]{1,0:T(8,128)(2,1)S(1)} %add_convert_fusion.4.value_ref), channel_id=1, source_target_pairs={{0,16},{4,20},{8,24},{12,28},{16,0},{20,4},{24,8},{28,12},{1,17},{... | collective-permute-start | bytes 884744 | tf_op jit(solution)/shard_map/ppermute | solution.py:397
  384.3 24.5 %collective-permute-start.19 = (bf16[192,768]{1,0:T(8,128)(2,1)S(1)}, bf16[192,768]{1,0:T(8,128)(2,1)S(1)}, u32[]{:S(2)}, u32[]{:S(2)}) collective-permute-start(bf16[192,768]{1,0:T(8,128)(2,1)S(1)} %add_convert_fusion.6.value_ref), channel_id=1, source_target_pairs={{0,16},{4,20},{8,24},{12,28},{16,0},{20,4},{24,8},{28,12},{1,17},{... | collective-permute-start | bytes 884744 | tf_op jit(solution)/shard_map/ppermute | solution.py:397
  399.0 21.4 %collective-permute-start.26 = (bf16[384,768]{1,0:T(8,128)(2,1)}, bf16[384,768]{1,0:T(8,128)(2,1)S(1)}, u32[]{:S(2)}, u32[]{:S(2)}) collective-permute-start(bf16[384,768]{1,0:T(8,128)(2,1)} %join.10.value_ref), channel_id=1, source_target_pairs={{0,8},{4,12},{8,0},{12,4},{16,24},{20,28},{24,16},{28,20},{1,9},{5... | collective-permute-start | bytes 1769480 | tf_op jit(solution)/shard_map/ppermute | solution.py:397
  411.4 20.9 %collective-permute-start.20 = (bf16[384,768]{1,0:T(8,128)(2,1)}, bf16[384,768]{1,0:T(8,128)(2,1)S(1)}, u32[]{:S(2)}, u32[]{:S(2)}) collective-permute-start(bf16[384,768]{1,0:T(8,128)(2,1)} %join.8.value_ref), channel_id=1, source_target_pairs={{0,8},{4,12},{8,0},{12,4},{16,24},{20,28},{24,16},{28,20},{1,9},{5... | collective-permute-start | bytes 1769480 | tf_op jit(solution)/shard_map/ppermute | solution.py:397
  415.8 22.5 %collective-permute-start.15 = (bf16[864,256]{1,0:T(8,128)(2,1)}, bf16[864,256]{1,0:T(8,128)(2,1)S(1)}, u32[]{:S(2)}, u32[]{:S(2)}) collective-permute-start(bf16[864,256]{1,0:T(8,128)(2,1)} %join.7.value_ref), channel_id=1, source_target_pairs={{0,1},{1,0},{2,3},{3,2},{4,5},{5,4},{6,7},{7,6},{8,9},{9,8},{10,11... | collective-permute-start | bytes 1327112 | tf_op jit(solution)/shard_map/ppermute | solution.py:397
  423.5 32.4 %collective-permute-start.27 = (bf16[768,768]{1,0:T(8,128)(2,1)}, bf16[768,768]{1,0:T(8,128)(2,1)S(1)}, u32[]{:S(2)}, u32[]{:S(2)}) collective-permute-start(bf16[768,768]{1,0:T(8,128)(2,1)} %join.11.value_ref), channel_id=1, source_target_pairs={{0,4},{4,0},{8,12},{12,8},{16,20},{20,16},{24,28},{28,24},{1,5},{5... | collective-permute-start | bytes 3538952 | tf_op jit(solution)/shard_map/ppermute | solution.py:397
  435.4 40.1 %collective-permute-start.21 = (bf16[768,768]{1,0:T(8,128)(2,1)}, bf16[768,768]{1,0:T(8,128)(2,1)S(1)}, u32[]{:S(2)}, u32[]{:S(2)}) collective-permute-start(bf16[768,768]{1,0:T(8,128)(2,1)} %join.9.value_ref), channel_id=1, source_target_pairs={{0,4},{4,0},{8,12},{12,8},{16,20},{20,16},{24,28},{28,24},{1,5},{5... | collective-permute-start | bytes 3538952 | tf_op jit(solution)/shard_map/ppermute | solution.py:397
  (32 other events, 357.3 us)
Sparse Core Ops, SparseCore 0:
  175.1 113.3 all-reduce.8
Sparse Core Ops, SparseCore 1:
  222.8 72.8 all-gather.1

commit v2 on v1

--- a/solution.py
+++ b/solution.py
@@ -401,16 +401,15 @@
     return max(b for b in range(16, 513, 16) if rows % b == 0)
 
 
-def place(buffer, value, slot, dtype, mixed=False):
+def place(buffer, value, slot, dtype, parts):
     rows, width = value.shape
-    block = rows // 2 if mixed else block_of(rows)
+    block = block_of(rows)
     count = rows // block
-    where = (lambda i, s: (2 * i + s[0], 0)) if mixed else (lambda i, s: (s[0] * count + i, 0))
 
     def kernel(slot_ref, value_ref, *refs):
         refs[-1][...] = value_ref[...].astype(dtype)
 
-    out = jax.ShapeDtypeStruct((2 * rows, width), dtype)
+    out = jax.ShapeDtypeStruct((parts * rows, width), dtype)
     given = () if buffer is None else (buffer,)
     return pl.pallas_call(
         kernel,
@@ -419,7 +418,7 @@
             grid=(count,),
             in_specs=[pl.BlockSpec((block, width), lambda i, s: (i, 0))]
             + [pl.BlockSpec(memory_space=pl.ANY) for _ in given],
-            out_specs=pl.BlockSpec((block, width), where),
+            out_specs=pl.BlockSpec((block, width), lambda i, s: (s[0] * count + i, 0)),
         ),
         out_shape=out,
         input_output_aliases={2: 0} if given else {},
@@ -440,6 +439,29 @@
         out_shape=jax.ShapeDtypeStruct(value.shape, value.dtype),
         name="copy_rows",
     )(value)
+
+
+def assemble(pieces, slots, dtype):
+    rows, width = pieces[0].shape
+
+    def kernel(slots_ref, *refs):
+        for k, ref in enumerate(refs[:-1]):
+
+            @pl.when(pl.program_id(0) == k)
+            def _(ref=ref):
+                refs[-1][...] = ref[...].astype(dtype)
+
+    return pl.pallas_call(
+        kernel,
+        grid_spec=pltpu.PrefetchScalarGridSpec(
+            num_scalar_prefetch=1,
+            grid=(len(pieces),),
+            in_specs=[pl.BlockSpec((rows, width), lambda i, s: (0, 0)) for _ in pieces],
+            out_specs=pl.BlockSpec((rows, width), lambda i, s: (s[i], 0)),
+        ),
+        out_shape=jax.ShapeDtypeStruct((len(pieces) * rows, width), dtype),
+        name="assemble",
+    )(jnp.stack(slots).astype(jnp.int32), *pieces)
 
 
 def join(value, other, upper):
@@ -561,20 +583,35 @@
     return add_parts(parts, 0, rows)
 
 
+def rows_are_few(value):
+    return value.size * value.dtype.itemsize < 2**18
+
+
 def gather_rows(value, axis, size, dtype, mixed=False):
     index = lax.axis_index(axis)
     bits = bits_of(size)
-    if bits is None:
+    if bits is None or len(bits) < 2:
         return lax.all_gather(value, axis, axis=0, tiled=True).astype(dtype)
-    for bit in bits[::-1]:
+    for bit in bits[:1:-1]:
         other = swap(value, axis, size, bit)
-        upper = (index // bit) % 2
-        if bit == bits[0]:
-            buffer = place(None, value, upper, dtype, mixed)
-            value = place(buffer, other, 1 - upper, dtype, mixed)
-        else:
-            value = join(value, other, upper)
-    return value.astype(dtype)
+        value = join(value, other, (index // bit) % 2)
+    outer, inner = bits[:2]
+    near = swap(value, axis, size, inner)
+    far = swap(value, axis, size, outer)
+    both = swap(near, axis, size, outer)
+    side, half = (index // outer) % 2, (index // inner) % 2
+
+    def slot(flip_outer, flip_inner):
+        x, y = (1 - side if flip_outer else side), (1 - half if flip_inner else half)
+        return x + 2 * y if mixed else 2 * x + y
+
+    if rows_are_few(value):
+        pieces = (value, far, near, both)
+        return assemble(pieces, [slot(0, 0), slot(1, 0), slot(0, 1), slot(1, 1)], dtype)
+    buffer = None
+    for piece, flips in ((value, (0, 0)), (far, (1, 0)), (near, (0, 1)), (both, (1, 1))):
+        buffer = place(buffer, piece, slot(*flips), dtype, 4)
+    return buffer
 
 
 def reduce_rows(value, axis, size, dtype):

time: 500 us -> 484 us (0.968)
  waiting for transfers between devices: 175 us -> 156 us
    ppermute x28 -> x32, waiting for transfers between devices: 175 us -> 156 us  [swap(): return lax.ppermute(value, axis, [(i, i ^ bit) for i in range(size)])]
    pallas_call x6 -> x2, Pallas kernels: 13.8 us -> 3.79 us  [join(): pl.pallas_call(kernel, grid_spec=pltpu.PrefetchScalarGridSpec(num_scalar_...]
    pallas_call x8 -> x12, Pallas kernels: 20 us -> 27.8 us  [place(): pl.pallas_call(kernel, grid_spec=pltpu.PrefetchScalarGridSpec(num_scalar_...]
    ppermute x28 -> x32, starting transfers between devices: 29 us -> 28.2 us  [swap(): return lax.ppermute(value, axis, [(i, i ^ bit) for i in range(size)])]
  transfers between devices with their start and end apart: 30 -> 34, of which waited for: 14 -> 15; matrix products, arithmetic and copies ran while one was open for 14% -> 15% of each run, Pallas kernels for 9% -> 10%
where the time goes in v2:
time: 484 us; the launch traced here: 483 us
  Pallas kernels  196 us (40%)
  waiting for transfers between devices  156 us (32%)
  other arithmetic  35.9 us (7%)
  matrix products  28.9 us (6%)
  starting transfers between devices  28.3 us (6%)
  local copies, waits for them, and re-layouts  21.8 us (5%)
  between operations  15.8 us (3%)
    ppermute x32, waiting for transfers between devices, swap(): return lax.ppermute(value, axis, [(i, i ^ bit) for i in range(size)])  156 us
    pallas_call x1, Pallas kernels, on_device(): pl.pallas_call(lead_kernel, grid=(tokens // lead,), in_specs=[by_rows(mod...  55 us
    pallas_call x1, Pallas kernels, on_device(): pl.pallas_call(backward_kernel, grid=(seqs, per_seq), in_specs=[of(v) for...  47 us
    dot_general x3, matrix products, dot_tn(): lax.dot_general(a, b, (((0,), (0,)), ((), ())), preferred_element_type=f32)  28.9 us
    ppermute x32, starting transfers between devices, swap(): return lax.ppermute(value, axis, [(i, i ^ bit) for i in range(size)])  28.2 us
    pallas_call x12, Pallas kernels, place(): pl.pallas_call(kernel, grid_spec=pltpu.PrefetchScalarGridSpec(num_scalar_...  27.8 us
    pallas_call x1, Pallas kernels, on_device(): pl.pallas_call(group_kernel, grid_spec=pltpu.PrefetchScalarGridSpec(num_s...  21.5 us
    pallas_call x1, Pallas kernels, on_device(): pl.pallas_call(middle_kernel, grid_spec=pltpu.PrefetchScalarGridSpec(num_...  19.4 us
  transfers between devices with their start and end apart: 34, of which 15 were waited for; matrix products, arithmetic and copies ran while one was open for 15% of the time, Pallas kernels for 10%

profile of v2, /device:TPU:0, one launch (start us, length us, event | category | flops | bytes accessed | tf_op | source)
XLA Modules:
  0.0 482.9 jit_solution(17237498430338785059)
XLA Ops:
  14.6 55.0 %lead.1 = (bf16[2048,1536]{1,0:T(8,128)(2,1)}, bf16[2048,768]{1,0:T(8,128)(2,1)}, bf16[2048,1024]{1,0:T(8,128)(2,1)}, f32[2048,128]{1,0:T(8,128)}, bf16[2048,768...) custom-call(bf16[2048,1536]{1,0:T(8,128)(2,1)} %tokens_ref.5, ...), custom_call_target="tpu_custom_call" | custom-call | tf_op jit(solution)/shard_map/lead/pallas_call | solution.py:718
  69.5 3.1 collective-permute-start.1
  77.4 19.4 %middle.1 = (bf16[2048,768]{1,0:T(8,128)(2,1)}, bf16[2048,768]{1,0:T(8,128)(2,1)}, bf16[2048,768]{1,0:T(8,128)(2,1)}, bf16[1024,1536]{1,0:T(8,128)(2,1)}, bf16[1024,1536]{1,0:T(8,128)(2,1)}, /*index=5*/f32[16,768]{1,0:T(8,128)}) custom-call(s32[1]{0:T(128)} %bitcast.3._, bf16[2048,768]{1,0:T(8,128)(2,1)} %get-tuple-element.37.gate_ref, ...), custom_call_target="tpu_custom_call" | custom-call | tf_op jit(solution)/shard_map/middle/pallas_call | solution.py:763
  96.8 47.0 %ssd_backward.1 = (bf16[2048,1152]{1,0:T(8,128)(2,1)}, f32[48,1024]{1,0:T(8,128)}) custom-call(bf16[2048,768]{1,0:T(8,128)(2,1)} %get-tuple-element.45.mix_ref, f32[2048,768]{1,0:T(8,128)} %get-tuple-element.39.y_ref, bf16[2048,1024]{1,0:T(8,128)(2,1)} %get-tuple-element.40.act_ref, bf16[2048,1024]{1,0:T(8,128)(2,1)} %get-tuple-element.46.pre_ref, ...), custom_call_target="tpu_custom_call" | custom-call | tf_op jit(solution)/shard_map/ssd_backward/pallas_call | solution.py:806
  143.8 21.5 %group_in.1 = (bf16[1024,1536]{1,0:T(8,128)(2,1)}, bf16[1024,1536]{1,0:T(8,128)(2,1)}, f32[8,1536]{1,0:T(8,128)}) custom-call(s32[1]{0:T(128)} %bitcast.3._, bf16[2048,768]{1,0:T(8,128)(2,1)} %get-tuple-element.44.gate_ref, bf16[2048,1152]{1,0:T(8,128)(2,1)} %get-tuple-element.50.packed_ref, bf16[2048,1536]{1,0:T(8,128)(2,1)} %get-tuple-element.51.normed_ref, ...), custom_call_target="tpu_custom_call" | custom-call | tf_op jit(solution)/shard_map/group_in/pallas_call | solution.py:826
  165.4 9.5 %convolution_convert_fusion.1 = bf16[768,1536]{1,0:T(8,128)(2,1)} fusion(bf16[2048,768]{1,0:T(8,128)(2,1)} %get-tuple-element.57, bf16[2048,1536]{1,0:T(8,128)(2,1)} %grad_ref.1), kind=kOutput, calls=%fused_computation.1 | convolution fusion | flops 4833017856 | bytes 11796480 | tf_op jit(solution)/shard_map/dot_general | solution.py:32
  179.7 35.0 %collective-permute-done.9.last_ref = bf16[512,1536]{1,0:T(8,128)(2,1)S(1)} collective-permute-done((bf16[512,1536]{1,0:T(8,128)(2,1)}, bf16[512,1536]{1,0:T(8,128)(2,1)S(1)}, u32[]{:S(2)}, u32[]{:S(2)}) %collective-permute-start.9) | collective-permute-done | bytes 1572896 | tf_op jit(solution)/shard_map/ppermute | solution.py:397
  215.9 6.8 %quarter.3 = bf16[512,1536]{1,0:T(8,128)(2,1)} custom-call(s32[2]{0:T(128)} %pad_add_fusion._, bf16[1024,1536]{1,0:T(8,128)(2,1)} %get-tuple-element.52.kept_ref, bf16[1024,1536]{1,0:T(8,128)(2,1)} %collective-permute-done.8.other_ref, bf16[512,1536]{1,0:T(8,128)(2,1)} %copy-done.8, bf16[2048,1536]{1,0:T(8,128)(2,1)} %tokens_ref.5, ...), custom_call_target="tpu_custom_call" | custom-call | tf_op jit(solution)/shard_map/quarter/pallas_call | solution.py:518
  222.7 12.0 %convolution_convert_fusion = bf16[1536,1152]{1,0:T(8,128)(2,1)S(1)} fusion(bf16[2048,1536]{1,0:T(8,128)(2,1)} %get-tuple-element.51.normed_ref, bf16[2048,1152]{1,0:T(8,128)(2,1)} %get-tuple-element.50.packed_ref), kind=kOutput, calls=%fused_computation | convolution fusion | flops 7249526784 | bytes 14548992 | tf_op jit(solution)/shard_map/dot_general | solution.py:32
  239.2 7.4 %convolution_convert_fusion.2 = bf16[1536,768]{1,0:T(8,128)(2,1)S(1)} fusion(bf16[2048,1536]{1,0:T(8,128)(2,1)} %get-tuple-element.51.normed_ref, bf16[2048,768]{1,0:T(8,128)(2,1)S(1)} %copy-done.2), kind=kOutput, calls=%fused_computation.2 | convolution fusion | flops 4833017856 | bytes 11796480 | tf_op jit(solution)/shard_map/dot_general | solution.py:32
  255.5 3.8 add_convert_fusion.1
  260.5 7.3 %collective-permute-done.11 = bf16[432,256]{1,0:T(8,128)(2,1)S(1)} collective-permute-done((bf16[432,256]{1,0:T(8,128)(2,1)S(1)}, bf16[432,256]{1,0:T(8,128)(2,1)S(1)}, u32[]{:S(2)}, u32[]{:S(2)}) %collective-permute-start.11) | collective-permute-done | bytes 221216 | tf_op jit(solution)/shard_map/ppermute | solution.py:397
  270.8 36.5 %collective-permute-done.12 = bf16[92,1536]{1,0:T(8,128)(2,1)S(1)} collective-permute-done((bf16[92,1536]{1,0:T(8,128)(2,1)S(1)}, bf16[92,1536]{1,0:T(8,128)(2,1)S(1)}, u32[]{:S(2)}, u32[]{:S(2)}) %collective-permute-start.12) | collective-permute-done | bytes 282656 | tf_op jit(solution)/shard_map/ppermute | solution.py:397
  308.8 7.1 %collective-permute-done.13 = bf16[92,1536]{1,0:T(8,128)(2,1)S(1)} collective-permute-done((bf16[92,1536]{1,0:T(8,128)(2,1)S(1)}, bf16[92,1536]{1,0:T(8,128)(2,1)S(1)}, u32[]{:S(2)}, u32[]{:S(2)}) %collective-permute-start.13) | collective-permute-done | bytes 282656 | tf_op jit(solution)/shard_map/ppermute | solution.py:397
  324.0 5.4 %quarter.2.value_ref = bf16[512,1536]{1,0:T(8,128)(2,1)} custom-call(s32[2]{0:T(128)} %pad_add_fusion._, bf16[1024,1536]{1,0:T(8,128)(2,1)} %get-tuple-element.42.kept_ref, bf16[1024,1536]{1,0:T(8,128)(2,1)} %collective-permute-done.3.other_ref, bf16[512,1536]{1,0:T(8,128)(2,1)} %collective-permute-done.4.last_ref, bf16[2048,1536]{1,0:T(8,128)(2,1)} %tokens_ref.5), custom_call_target="tpu_custom_call" | custom-call | tf_op jit(solution)/shard_map/quarter/pallas_call | solution.py:518
  334.5 6.9 %collective-permute-done.26 = bf16[384,768]{1,0:T(8,128)(2,1)} collective-permute-done((bf16[384,768]{1,0:T(8,128)(2,1)S(1)}, bf16[384,768]{1,0:T(8,128)(2,1)}, u32[]{:S(2)}, u32[]{:S(2)}) %collective-permute-start.26) | collective-permute-done | bytes 589856 | tf_op jit(solution)/shard_map/ppermute | solution.py:397
  342.9 15.0 %collective-permute-done.19 = bf16[384,768]{1,0:T(8,128)(2,1)} collective-permute-done((bf16[384,768]{1,0:T(8,128)(2,1)}, bf16[384,768]{1,0:T(8,128)(2,1)}, u32[]{:S(2)}, u32[]{:S(2)}) %collective-permute-start.19) | collective-permute-done | bytes 589856 | tf_op jit(solution)/shard_map/ppermute | solution.py:397
  364.5 14.7 %collective-permute-done.20 = bf16[192,768]{1,0:T(8,128)(2,1)S(1)} collective-permute-done((bf16[192,768]{1,0:T(8,128)(2,1)S(1)}, bf16[192,768]{1,0:T(8,128)(2,1)S(1)}, u32[]{:S(2)}, u32[]{:S(2)}) %collective-permute-start.20) | collective-permute-done | bytes 294944 | tf_op jit(solution)/shard_map/ppermute | solution.py:397
  382.5 9.4 %collective-permute-done.28.other_ref = bf16[192,768]{1,0:T(8,128)(2,1)} collective-permute-done((bf16[192,768]{1,0:T(8,128)(2,1)S(1)}, bf16[192,768]{1,0:T(8,128)(2,1)}, u32[]{:S(2)}, u32[]{:S(2)}) %collective-permute-start.28) | collective-permute-done | bytes 294944 | tf_op jit(solution)/shard_map/ppermute | solution.py:397
  403.7 3.4 assemble.1
  407.8 5.9 %collective-permute-done.31.value_ref = bf16[384,768]{1,0:T(8,128)(2,1)} collective-permute-done((bf16[384,768]{1,0:T(8,128)(2,1)}, bf16[384,768]{1,0:T(8,128)(2,1)}, u32[]{:S(2)}, u32[]{:S(2)}) %collective-permute-start.31) | collective-permute-done | bytes 589856 | tf_op jit(solution)/shard_map/ppermute | solution.py:397
  418.6 9.7 %collective-permute-done.22.value_ref = bf16[384,768]{1,0:T(8,128)(2,1)} collective-permute-done((bf16[384,768]{1,0:T(8,128)(2,1)}, bf16[384,768]{1,0:T(8,128)(2,1)}, u32[]{:S(2)}, u32[]{:S(2)}) %collective-permute-start.22) | collective-permute-done | bytes 589856 | tf_op jit(solution)/shard_map/ppermute | solution.py:397
  439.2 4.5 convert_element_type.240
  469.5 5.9 %copy_rows.1 = bf16[2048,1536]{1,0:T(8,128)(2,1)} custom-call(bf16[2048,1536]{1,0:T(8,128)(2,1)} %all-gather.2.cloned.1.call-done.value_ref), custom_call_target="tpu_custom_call" | custom-call | tf_op jit(solution)/shard_map/copy_rows/pallas_call | solution.py:434
  (174 shorter events, 115.0 us)
Async XLA Ops:
  8.0 431.2 %all-reduce.9.cloned.1.call-start = ((), (), s32[]{:S(2)}) async-start(), calls=%async_computation.1 | async-start | bytes 4718592 | tf_op jit(solution)/shard_map/psum | solution.py:779
  174.9 294.6 %all-gather.2.cloned.1.call-start = ((), (), s32[]{:S(2)}) async-start(), calls=%async_computation | async-start | bytes 7864320 | tf_op jit(solution)/shard_map/all_gather | solution.py:857
  178.0 36.8 %collective-permute-start.9 = (bf16[512,1536]{1,0:T(8,128)(2,1)}, bf16[512,1536]{1,0:T(8,128)(2,1)S(1)}, u32[]{:S(2)}, u32[]{:S(2)}) collective-permute-start(bf16[512,1536]{1,0:T(8,128)(2,1)} %add_convert_fusion), channel_id=1, source_target_pairs={{0,2},{1,3},{2,0},{3,1},{4,6},{5,7},{6,4},{7,5},{8,10},{9,11},{10,... | collective-permute-start | bytes 4718600 | tf_op jit(solution)/shard_map/ppermute | solution.py:397
  179.7 75.8 %collective-permute-start.3 = (bf16[1024,1536]{1,0:T(8,128)(2,1)}, bf16[1024,1536]{1,0:T(8,128)(2,1)}, u32[]{:S(2)}, u32[]{:S(2)}) collective-permute-start(bf16[1024,1536]{1,0:T(8,128)(2,1)} %get-tuple-element.43), channel_id=1, source_target_pairs={{0,1},{1,0},{2,3},{3,2},{4,5},{5,4},{6,7},{7,6},{8,9},{9,8},{10,11... | collective-permute-start | bytes 9437192 | tf_op jit(solution)/shard_map/ppermute | solution.py:397
  237.7 80.8 %collective-permute-start.25 = (bf16[768,768]{1,0:T(8,128)(2,1)}, bf16[768,768]{1,0:T(8,128)(2,1)}, u32[]{:S(2)}, u32[]{:S(2)}) collective-permute-start(bf16[768,768]{1,0:T(8,128)(2,1)} %constant_dynamic-slice_fusion.1), channel_id=1, source_target_pairs={{0,4},{4,0},{8,12},{12,8},{16,20},{20,16},{24,28},{28,24},{1,5},{5... | collective-permute-start | bytes 3538952 | tf_op jit(solution)/shard_map/ppermute | solution.py:397
  249.1 72.1 %collective-permute-start.18 = (bf16[768,768]{1,0:T(8,128)(2,1)}, bf16[768,768]{1,0:T(8,128)(2,1)}, u32[]{:S(2)}, u32[]{:S(2)}) collective-permute-start(bf16[768,768]{1,0:T(8,128)(2,1)} %constant_dynamic-slice_fusion), channel_id=1, source_target_pairs={{0,4},{4,0},{8,12},{12,8},{16,20},{20,16},{24,28},{28,24},{1,5},{5... | collective-permute-start | bytes 3538952 | tf_op jit(solution)/shard_map/ppermute | solution.py:397
  259.3 64.7 %collective-permute-start.4 = (bf16[512,1536]{1,0:T(8,128)(2,1)}, bf16[512,1536]{1,0:T(8,128)(2,1)}, u32[]{:S(2)}, u32[]{:S(2)}) collective-permute-start(bf16[512,1536]{1,0:T(8,128)(2,1)} %add_convert_fusion.1), channel_id=1, source_target_pairs={{0,2},{1,3},{2,0},{3,1},{4,6},{5,7},{6,4},{7,5},{8,10},{9,11},{10,... | collective-permute-start | bytes 4718600 | tf_op jit(solution)/shard_map/ppermute | solution.py:397
  269.4 37.8 %collective-permute-start.12 = (bf16[92,1536]{1,0:T(8,128)(2,1)S(1)}, bf16[92,1536]{1,0:T(8,128)(2,1)S(1)}, u32[]{:S(2)}, u32[]{:S(2)}) collective-permute-start(bf16[92,1536]{1,0:T(8,128)(2,1)S(1)} %fusion.4), channel_id=1, source_target_pairs={{0,4},{4,0},{8,12},{12,8},{16,20},{20,16},{24,28},{28,24},{1,5},{5... | collective-permute-start | bytes 847880 | tf_op jit(solution)/shard_map/ppermute | solution.py:397
  319.7 21.7 %collective-permute-start.26 = (bf16[384,768]{1,0:T(8,128)(2,1)S(1)}, bf16[384,768]{1,0:T(8,128)(2,1)}, u32[]{:S(2)}, u32[]{:S(2)}) collective-permute-start(bf16[384,768]{1,0:T(8,128)(2,1)S(1)} %add_convert_fusion.2), channel_id=1, source_target_pairs={{0,8},{4,12},{8,0},{12,4},{16,24},{20,28},{24,16},{28,20},{1,9},{5... | collective-permute-start | bytes 1769480 | tf_op jit(solution)/shard_map/ppermute | solution.py:397
  323.4 34.4 %collective-permute-start.19 = (bf16[384,768]{1,0:T(8,128)(2,1)}, bf16[384,768]{1,0:T(8,128)(2,1)}, u32[]{:S(2)}, u32[]{:S(2)}) collective-permute-start(bf16[384,768]{1,0:T(8,128)(2,1)} %add_convert_fusion.3), channel_id=1, source_target_pairs={{0,8},{4,12},{8,0},{12,4},{16,24},{20,28},{24,16},{28,20},{1,9},{5... | collective-permute-start | bytes 1769480 | tf_op jit(solution)/shard_map/ppermute | solution.py:397
  329.4 62.6 %collective-permute-start.5 = (bf16[512,1536]{1,0:T(8,128)(2,1)}, bf16[512,1536]{1,0:T(8,128)(2,1)}, u32[]{:S(2)}, u32[]{:S(2)}) collective-permute-start(bf16[512,1536]{1,0:T(8,128)(2,1)} %quarter.2.value_ref), channel_id=1, source_target_pairs={{0,2},{1,3},{2,0},{3,1},{4,6},{5,7},{6,4},{7,5},{8,10},{9,11},{10,... | collective-permute-start | bytes 4718600 | tf_op jit(solution)/shard_map/ppermute | solution.py:397
  333.3 49.2 %collective-permute-start.16 = (bf16[432,256]{1,0:T(8,128)(2,1)}, bf16[432,256]{1,0:T(8,128)(2,1)}, u32[]{:S(2)}, u32[]{:S(2)}) collective-permute-start(bf16[432,256]{1,0:T(8,128)(2,1)} %reshape.215.refs_0_), channel_id=1, source_target_pairs={{0,2},{1,3},{2,0},{3,1},{4,6},{5,7},{6,4},{7,5},{8,10},{9,11},{10,... | collective-permute-start | bytes 663560 | tf_op jit(solution)/shard_map/ppermute | solution.py:397
  334.5 65.6 %collective-permute-start.15 = (bf16[432,256]{1,0:T(8,128)(2,1)}, bf16[432,256]{1,0:T(8,128)(2,1)}, u32[]{:S(2)}, u32[]{:S(2)}) collective-permute-start(bf16[432,256]{1,0:T(8,128)(2,1)} %reshape.215.refs_0_), channel_id=1, source_target_pairs={{0,1},{1,0},{2,3},{3,2},{4,5},{5,4},{6,7},{7,6},{8,9},{9,8},{10,11... | collective-permute-start | bytes 663560 | tf_op jit(solution)/shard_map/ppermute | solution.py:397
  342.5 18.3 %collective-permute-start.27 = (bf16[192,768]{1,0:T(8,128)(2,1)S(1)}, bf16[192,768]{1,0:T(8,128)(2,1)S(1)}, u32[]{:S(2)}, u32[]{:S(2)}) collective-permute-start(bf16[192,768]{1,0:T(8,128)(2,1)S(1)} %add_convert_fusion.5), channel_id=1, source_target_pairs={{0,16},{4,20},{8,24},{12,28},{16,0},{20,4},{24,8},{28,12},{1,17},{... | collective-permute-start | bytes 884744 | tf_op jit(solution)/shard_map/ppermute | solution.py:397
  359.1 20.1 %collective-permute-start.20 = (bf16[192,768]{1,0:T(8,128)(2,1)S(1)}, bf16[192,768]{1,0:T(8,128)(2,1)S(1)}, u32[]{:S(2)}, u32[]{:S(2)}) collective-permute-start(bf16[192,768]{1,0:T(8,128)(2,1)S(1)} %add_convert_fusion.7), channel_id=1, source_target_pairs={{0,16},{4,20},{8,24},{12,28},{16,0},{20,4},{24,8},{28,12},{1,17},{... | collective-permute-start | bytes 884744 | tf_op jit(solution)/shard_map/ppermute | solution.py:397
  362.0 29.9 %collective-permute-start.28 = (bf16[192,768]{1,0:T(8,128)(2,1)S(1)}, bf16[192,768]{1,0:T(8,128)(2,1)}, u32[]{:S(2)}, u32[]{:S(2)}) collective-permute-start(bf16[192,768]{1,0:T(8,128)(2,1)S(1)} %add_convert_fusion.4.value_ref), channel_id=1, source_target_pairs={{0,16},{4,20},{8,24},{12,28},{16,0},{20,4},{24,8},{28,12},{1,17},{... | collective-permute-start | bytes 884744 | tf_op jit(solution)/shard_map/ppermute | solution.py:397
  381.2 17.0 %collective-permute-start.21 = (bf16[192,768]{1,0:T(8,128)(2,1)}, bf16[192,768]{1,0:T(8,128)(2,1)}, u32[]{:S(2)}, u32[]{:S(2)}) collective-permute-start(bf16[192,768]{1,0:T(8,128)(2,1)} %add_convert_fusion.6.value_ref), channel_id=1, source_target_pairs={{0,16},{4,20},{8,24},{12,28},{16,0},{20,4},{24,8},{28,12},{1,17},{... | collective-permute-start | bytes 884744 | tf_op jit(solution)/shard_map/ppermute | solution.py:397
  382.5 17.6 %collective-permute-start.17 = (bf16[432,256]{1,0:T(8,128)(2,1)}, bf16[432,256]{1,0:T(8,128)(2,1)}, u32[]{:S(2)}, u32[]{:S(2)}) collective-permute-start(bf16[432,256]{1,0:T(8,128)(2,1)} %collective-permute-done.16.refs_2_), channel_id=1, source_target_pairs={{0,1},{1,0},{2,3},{3,2},{4,5},{5,4},{6,7},{7,6},{8,9},{9,8},{10,11... | collective-permute-start | bytes 663560 | tf_op jit(solution)/shard_map/ppermute | solution.py:397
  392.0 67.3 %collective-permute-start.7 = (bf16[512,1536]{1,0:T(8,128)(2,1)}, bf16[512,1536]{1,0:T(8,128)(2,1)S(1)}, u32[]{:S(2)}, u32[]{:S(2)}) collective-permute-start(bf16[512,1536]{1,0:T(8,128)(2,1)} %quarter.2.value_ref), channel_id=1, source_target_pairs={{0,1},{1,0},{2,3},{3,2},{4,5},{5,4},{6,7},{7,6},{8,9},{9,8},{10,11... | collective-permute-start | bytes 4718600 | tf_op jit(solution)/shard_map/ppermute | solution.py:397
  392.0 73.8 %collective-permute-start.6 = (bf16[512,1536]{1,0:T(8,128)(2,1)}, bf16[512,1536]{1,0:T(8,128)(2,1)S(1)}, u32[]{:S(2)}, u32[]{:S(2)}) collective-permute-start(bf16[512,1536]{1,0:T(8,128)(2,1)} %collective-permute-done.5.value_ref), channel_id=1, source_target_pairs={{0,1},{1,0},{2,3},{3,2},{4,5},{5,4},{6,7},{7,6},{8,9},{9,8},{10,11... | collective-permute-start | bytes 4718600 | tf_op jit(solution)/shard_map/ppermute | solution.py:397
  400.1 28.2 %collective-permute-start.22 = (bf16[384,768]{1,0:T(8,128)(2,1)}, bf16[384,768]{1,0:T(8,128)(2,1)}, u32[]{:S(2)}, u32[]{:S(2)}) collective-permute-start(bf16[384,768]{1,0:T(8,128)(2,1)} %join.2.value_ref), channel_id=1, source_target_pairs={{0,8},{4,12},{8,0},{12,4},{16,24},{20,28},{24,16},{28,20},{1,9},{5... | collective-permute-start | bytes 1769480 | tf_op jit(solution)/shard_map/ppermute | solution.py:397
  413.7 34.3 %collective-permute-start.24 = (bf16[384,768]{1,0:T(8,128)(2,1)}, bf16[384,768]{1,0:T(8,128)(2,1)}, u32[]{:S(2)}, u32[]{:S(2)}) collective-permute-start(bf16[384,768]{1,0:T(8,128)(2,1)} %join.2.value_ref), channel_id=1, source_target_pairs={{0,4},{4,0},{8,12},{12,8},{16,20},{20,16},{24,28},{28,24},{1,5},{5... | collective-permute-start | bytes 1769480 | tf_op jit(solution)/shard_map/ppermute | solution.py:397
  416.6 35.7 %collective-permute-start.30 = (bf16[384,768]{1,0:T(8,128)(2,1)}, bf16[384,768]{1,0:T(8,128)(2,1)}, u32[]{:S(2)}, u32[]{:S(2)}) collective-permute-start(bf16[384,768]{1,0:T(8,128)(2,1)} %collective-permute-done.29.value_ref), channel_id=1, source_target_pairs={{0,4},{4,0},{8,12},{12,8},{16,20},{20,16},{24,28},{28,24},{1,5},{5... | collective-permute-start | bytes 1769480 | tf_op jit(solution)/shard_map/ppermute | solution.py:397
  428.3 26.2 %collective-permute-start.23 = (bf16[384,768]{1,0:T(8,128)(2,1)}, bf16[384,768]{1,0:T(8,128)(2,1)}, u32[]{:S(2)}, u32[]{:S(2)}) collective-permute-start(bf16[384,768]{1,0:T(8,128)(2,1)} %collective-permute-done.22.value_ref), channel_id=1, source_target_pairs={{0,4},{4,0},{8,12},{12,8},{16,20},{20,16},{24,28},{28,24},{1,5},{5... | collective-permute-start | bytes 1769480 | tf_op jit(solution)/shard_map/ppermute | solution.py:397
  (27 other events, 293.3 us)
Sparse Core Ops, SparseCore 0:
  175.1 114.3 all-reduce.8
Sparse Core Ops, SparseCore 1:
  222.8 56.8 all-gather.1

commit v3 on v2

--- a/solution.py
+++ b/solution.py
@@ -123,17 +123,13 @@
         ext_ref[0:8, :] = jnp.zeros_like(ext_ref[0:8, :])
 
     part = 32
-
-    def normalize(index, carry):
-        r = pl.ds(pl.multiple_of(index * part, part), part)
+    for lo in range(0, rows, part):
+        r = slice(lo, lo + part)
         hidden = tokens_ref[r, :].astype(f32)
         inv = lax.rsqrt(jnp.mean(hidden * hidden, axis=1, keepdims=True) + eps_value)
         for k in range(pg_ref.shape[0]):
             c = slice(k * LANES, (k + 1) * LANES)
             normed_ref[r, c] = (hidden[:, c] * inv * pg_ref[k : k + 1, :]).astype(bf16)
-        return carry
-
-    lax.fori_loop(0, rows // part, normalize, 0)
     z = dot_nt(normed_ref[...], step_w[...])
     z_ref[...] = jnp.zeros_like(z_ref)
     z_ref[:, : z.shape[1]] = z
@@ -511,10 +507,11 @@
     quarter, width = kept.shape[0] // 2, kept.shape[1]
     out = add_parts([(kept, 0), (other, 0)], (1 - upper) * quarter, quarter).astype(kept.dtype)
     last = swap(out, "tensor", 4, 2)
-    count = quarter // T
-    half = pl.BlockSpec((T, width), lambda i, s: (s[1] * count + i, 0))
-    own = pl.BlockSpec((T, width), lambda i, s: (s[0] * count + i, 0))
-    plain = pl.BlockSpec((T, width), lambda i, s: (i, 0))
+    block = 2 * T if quarter % (2 * T) == 0 else T
+    count = quarter // block
+    half = pl.BlockSpec((block, width), lambda i, s: (s[1] * count + i, 0))
+    own = pl.BlockSpec((block, width), lambda i, s: (s[0] * count + i, 0))
+    plain = pl.BlockSpec((block, width), lambda i, s: (i, 0))
     return pl.pallas_call(
         kernel,
         grid_spec=pltpu.PrefetchScalarGridSpec(
@@ -536,7 +533,7 @@
 
 
 def input_kernel(_, kept_ref, other_ref, last_ref, tokens_ref, grad_ref, gain_ref, out_ref):
-    part = 32
+    part = 64
 
     def one(index, carry):
         r = pl.ds(pl.multiple_of(index * part, part), part)

time: 484 us -> 478 us (0.988)
  Pallas kernels: 196 us -> 188 us
    pallas_call x1, Pallas kernels: 55 us -> 48.8 us  [on_device(): pl.pallas_call(lead_kernel, grid=(tokens // lead,), in_specs=[by_rows(mod...]
  transfers between devices with their start and end apart: 34 -> 34, of which waited for: 15 -> 16; matrix products, arithmetic and copies ran while one was open for 15% -> 15% of each run, Pallas kernels for 10% -> 10%
where the time goes in v3:
time: 478 us; the launch traced here: 477 us
  Pallas kernels  188 us (39%)
  waiting for transfers between devices  158 us (33%)
  other arithmetic  35.6 us (7%)
  matrix products  28.9 us (6%)
  starting transfers between devices  28.6 us (6%)
  local copies, waits for them, and re-layouts  21.8 us (5%)
  between operations  15.8 us (3%)
    ppermute x32, waiting for transfers between devices, swap(): return lax.ppermute(value, axis, [(i, i ^ bit) for i in range(size)])  158 us
    pallas_call x1, Pallas kernels, on_device(): pl.pallas_call(lead_kernel, grid=(tokens // lead,), in_specs=[by_rows(mod...  48.8 us
    pallas_call x1, Pallas kernels, on_device(): pl.pallas_call(backward_kernel, grid=(seqs, per_seq), in_specs=[of(v) for...  47 us
    dot_general x3, matrix products, dot_tn(): lax.dot_general(a, b, (((0,), (0,)), ((), ())), preferred_element_type=f32)  28.9 us
    ppermute x32, starting transfers between devices, swap(): return lax.ppermute(value, axis, [(i, i ^ bit) for i in range(size)])  28.5 us
    pallas_call x12, Pallas kernels, place(): pl.pallas_call(kernel, grid_spec=pltpu.PrefetchScalarGridSpec(num_scalar_...  27.8 us
    pallas_call x1, Pallas kernels, on_device(): pl.pallas_call(group_kernel, grid_spec=pltpu.PrefetchScalarGridSpec(num_s...  21.5 us
    pallas_call x1, Pallas kernels, on_device(): pl.pallas_call(middle_kernel, grid_spec=pltpu.PrefetchScalarGridSpec(num_...  19.4 us
  transfers between devices with their start and end apart: 34, of which 16 were waited for; matrix products, arithmetic and copies ran while one was open for 15% of the time, Pallas kernels for 10%

profile of v3, /device:TPU:0, one launch (start us, length us, event | category | flops | bytes accessed | tf_op | source)
XLA Modules:
  0.0 476.5 jit_solution(11306870485484627296)
XLA Ops:
  14.6 48.8 %lead.1 = (bf16[2048,1536]{1,0:T(8,128)(2,1)}, bf16[2048,768]{1,0:T(8,128)(2,1)}, bf16[2048,1024]{1,0:T(8,128)(2,1)}, f32[2048,128]{1,0:T(8,128)}, bf16[2048,768...) custom-call(bf16[2048,1536]{1,0:T(8,128)(2,1)} %tokens_ref.5, ...), custom_call_target="tpu_custom_call" | custom-call | tf_op jit(solution)/shard_map/lead/pallas_call | solution.py:715
  63.3 3.1 collective-permute-start.1
  71.2 19.4 %middle.1 = (bf16[2048,768]{1,0:T(8,128)(2,1)}, bf16[2048,768]{1,0:T(8,128)(2,1)}, bf16[2048,768]{1,0:T(8,128)(2,1)}, bf16[1024,1536]{1,0:T(8,128)(2,1)}, bf16[1024,1536]{1,0:T(8,128)(2,1)}, /*index=5*/f32[16,768]{1,0:T(8,128)}) custom-call(s32[1]{0:T(128)} %bitcast.3._, bf16[2048,768]{1,0:T(8,128)(2,1)} %get-tuple-element.37.gate_ref, ...), custom_call_target="tpu_custom_call" | custom-call | tf_op jit(solution)/shard_map/middle/pallas_call | solution.py:760
  90.6 47.0 %ssd_backward.1 = (bf16[2048,1152]{1,0:T(8,128)(2,1)}, f32[48,1024]{1,0:T(8,128)}) custom-call(bf16[2048,768]{1,0:T(8,128)(2,1)} %get-tuple-element.45.mix_ref, f32[2048,768]{1,0:T(8,128)} %get-tuple-element.39.y_ref, bf16[2048,1024]{1,0:T(8,128)(2,1)} %get-tuple-element.40.act_ref, bf16[2048,1024]{1,0:T(8,128)(2,1)} %get-tuple-element.46.pre_ref, ...), custom_call_target="tpu_custom_call" | custom-call | tf_op jit(solution)/shard_map/ssd_backward/pallas_call | solution.py:803
  137.6 21.5 %group_in.1 = (bf16[1024,1536]{1,0:T(8,128)(2,1)}, bf16[1024,1536]{1,0:T(8,128)(2,1)}, f32[8,1536]{1,0:T(8,128)}) custom-call(s32[1]{0:T(128)} %bitcast.3._, bf16[2048,768]{1,0:T(8,128)(2,1)} %get-tuple-element.44.gate_ref, bf16[2048,1152]{1,0:T(8,128)(2,1)} %get-tuple-element.50.packed_ref, bf16[2048,1536]{1,0:T(8,128)(2,1)} %get-tuple-element.51.normed_ref, ...), custom_call_target="tpu_custom_call" | custom-call | tf_op jit(solution)/shard_map/group_in/pallas_call | solution.py:823
  159.2 9.5 %convolution_convert_fusion.1 = bf16[768,1536]{1,0:T(8,128)(2,1)} fusion(bf16[2048,768]{1,0:T(8,128)(2,1)} %get-tuple-element.57, bf16[2048,1536]{1,0:T(8,128)(2,1)} %grad_ref.1), kind=kOutput, calls=%fused_computation.1 | convolution fusion | flops 4833017856 | bytes 11796480 | tf_op jit(solution)/shard_map/dot_general | solution.py:32
  173.5 35.0 %collective-permute-done.9.last_ref = bf16[512,1536]{1,0:T(8,128)(2,1)S(1)} collective-permute-done((bf16[512,1536]{1,0:T(8,128)(2,1)}, bf16[512,1536]{1,0:T(8,128)(2,1)S(1)}, u32[]{:S(2)}, u32[]{:S(2)}) %collective-permute-start.9) | collective-permute-done | bytes 1572896 | tf_op jit(solution)/shard_map/ppermute | solution.py:393
  209.7 5.8 %quarter.3 = bf16[512,1536]{1,0:T(8,128)(2,1)} custom-call(s32[2]{0:T(128)} %pad_add_fusion._, bf16[1024,1536]{1,0:T(8,128)(2,1)} %get-tuple-element.52.kept_ref, bf16[1024,1536]{1,0:T(8,128)(2,1)} %collective-permute-done.8.other_ref, bf16[512,1536]{1,0:T(8,128)(2,1)} %copy-done.8, bf16[2048,1536]{1,0:T(8,128)(2,1)} %tokens_ref.5, ...), custom_call_target="tpu_custom_call" | custom-call | tf_op jit(solution)/shard_map/quarter/pallas_call | solution.py:515
  215.6 12.0 %convolution_convert_fusion = bf16[1536,1152]{1,0:T(8,128)(2,1)S(1)} fusion(bf16[2048,1536]{1,0:T(8,128)(2,1)} %get-tuple-element.51.normed_ref, bf16[2048,1152]{1,0:T(8,128)(2,1)} %get-tuple-element.50.packed_ref), kind=kOutput, calls=%fused_computation | convolution fusion | flops 7249526784 | bytes 14548992 | tf_op jit(solution)/shard_map/dot_general | solution.py:32
  232.1 7.4 %convolution_convert_fusion.2 = bf16[1536,768]{1,0:T(8,128)(2,1)S(1)} fusion(bf16[2048,1536]{1,0:T(8,128)(2,1)} %get-tuple-element.51.normed_ref, bf16[2048,768]{1,0:T(8,128)(2,1)S(1)} %copy-done.2), kind=kOutput, calls=%fused_computation.2 | convolution fusion | flops 4833017856 | bytes 11796480 | tf_op jit(solution)/shard_map/dot_general | solution.py:32
  248.4 3.5 add_convert_fusion.1
  253.1 7.6 %collective-permute-done.11 = bf16[432,256]{1,0:T(8,128)(2,1)S(1)} collective-permute-done((bf16[432,256]{1,0:T(8,128)(2,1)S(1)}, bf16[432,256]{1,0:T(8,128)(2,1)S(1)}, u32[]{:S(2)}, u32[]{:S(2)}) %collective-permute-start.11) | collective-permute-done | bytes 221216 | tf_op jit(solution)/shard_map/ppermute | solution.py:393
  263.6 37.4 %collective-permute-done.12 = bf16[92,1536]{1,0:T(8,128)(2,1)S(1)} collective-permute-done((bf16[92,1536]{1,0:T(8,128)(2,1)S(1)}, bf16[92,1536]{1,0:T(8,128)(2,1)S(1)}, u32[]{:S(2)}, u32[]{:S(2)}) %collective-permute-start.12) | collective-permute-done | bytes 282656 | tf_op jit(solution)/shard_map/ppermute | solution.py:393
  302.6 7.0 %collective-permute-done.13 = bf16[92,1536]{1,0:T(8,128)(2,1)S(1)} collective-permute-done((bf16[92,1536]{1,0:T(8,128)(2,1)S(1)}, bf16[92,1536]{1,0:T(8,128)(2,1)S(1)}, u32[]{:S(2)}, u32[]{:S(2)}) %collective-permute-start.13) | collective-permute-done | bytes 282656 | tf_op jit(solution)/shard_map/ppermute | solution.py:393
  317.7 4.7 quarter.2.value_ref
  328.3 6.8 %collective-permute-done.26 = bf16[384,768]{1,0:T(8,128)(2,1)} collective-permute-done((bf16[384,768]{1,0:T(8,128)(2,1)S(1)}, bf16[384,768]{1,0:T(8,128)(2,1)}, u32[]{:S(2)}, u32[]{:S(2)}) %collective-permute-start.26) | collective-permute-done | bytes 589856 | tf_op jit(solution)/shard_map/ppermute | solution.py:393
  336.7 14.9 %collective-permute-done.19 = bf16[384,768]{1,0:T(8,128)(2,1)} collective-permute-done((bf16[384,768]{1,0:T(8,128)(2,1)}, bf16[384,768]{1,0:T(8,128)(2,1)}, u32[]{:S(2)}, u32[]{:S(2)}) %collective-permute-start.19) | collective-permute-done | bytes 589856 | tf_op jit(solution)/shard_map/ppermute | solution.py:393
  358.2 14.6 %collective-permute-done.20 = bf16[192,768]{1,0:T(8,128)(2,1)S(1)} collective-permute-done((bf16[192,768]{1,0:T(8,128)(2,1)S(1)}, bf16[192,768]{1,0:T(8,128)(2,1)S(1)}, u32[]{:S(2)}, u32[]{:S(2)}) %collective-permute-start.20) | collective-permute-done | bytes 294944 | tf_op jit(solution)/shard_map/ppermute | solution.py:393
  376.2 9.4 %collective-permute-done.28.other_ref = bf16[192,768]{1,0:T(8,128)(2,1)} collective-permute-done((bf16[192,768]{1,0:T(8,128)(2,1)S(1)}, bf16[192,768]{1,0:T(8,128)(2,1)}, u32[]{:S(2)}, u32[]{:S(2)}) %collective-permute-start.28) | collective-permute-done | bytes 294944 | tf_op jit(solution)/shard_map/ppermute | solution.py:393
  398.0 3.4 assemble.1
  402.2 5.2 %collective-permute-done.31.value_ref = bf16[384,768]{1,0:T(8,128)(2,1)} collective-permute-done((bf16[384,768]{1,0:T(8,128)(2,1)}, bf16[384,768]{1,0:T(8,128)(2,1)}, u32[]{:S(2)}, u32[]{:S(2)}) %collective-permute-start.31) | collective-permute-done | bytes 589856 | tf_op jit(solution)/shard_map/ppermute | solution.py:393
  412.3 10.1 %collective-permute-done.22.value_ref = bf16[384,768]{1,0:T(8,128)(2,1)} collective-permute-done((bf16[384,768]{1,0:T(8,128)(2,1)}, bf16[384,768]{1,0:T(8,128)(2,1)}, u32[]{:S(2)}, u32[]{:S(2)}) %collective-permute-start.22) | collective-permute-done | bytes 589856 | tf_op jit(solution)/shard_map/ppermute | solution.py:393
  432.8 4.5 convert_element_type.240
  463.1 5.9 %copy_rows.1 = bf16[2048,1536]{1,0:T(8,128)(2,1)} custom-call(bf16[2048,1536]{1,0:T(8,128)(2,1)} %all-gather.2.cloned.1.call-done.value_ref), custom_call_target="tpu_custom_call" | custom-call | tf_op jit(solution)/shard_map/copy_rows/pallas_call | solution.py:430
  (174 shorter events, 115.9 us)
Async XLA Ops:
  8.0 424.8 %all-reduce.9.cloned.1.call-start = ((), (), s32[]{:S(2)}) async-start(), calls=%async_computation.1 | async-start | bytes 4718592 | tf_op jit(solution)/shard_map/psum | solution.py:776
  168.7 294.4 %all-gather.2.cloned.1.call-start = ((), (), s32[]{:S(2)}) async-start(), calls=%async_computation | async-start | bytes 7864320 | tf_op jit(solution)/shard_map/all_gather | solution.py:854
  171.8 36.8 %collective-permute-start.9 = (bf16[512,1536]{1,0:T(8,128)(2,1)}, bf16[512,1536]{1,0:T(8,128)(2,1)S(1)}, u32[]{:S(2)}, u32[]{:S(2)}) collective-permute-start(bf16[512,1536]{1,0:T(8,128)(2,1)} %add_convert_fusion), channel_id=1, source_target_pairs={{0,2},{1,3},{2,0},{3,1},{4,6},{5,7},{6,4},{7,5},{8,10},{9,11},{10,... | collective-permute-start | bytes 4718600 | tf_op jit(solution)/shard_map/ppermute | solution.py:393
  173.5 74.9 %collective-permute-start.3 = (bf16[1024,1536]{1,0:T(8,128)(2,1)}, bf16[1024,1536]{1,0:T(8,128)(2,1)}, u32[]{:S(2)}, u32[]{:S(2)}) collective-permute-start(bf16[1024,1536]{1,0:T(8,128)(2,1)} %get-tuple-element.43), channel_id=1, source_target_pairs={{0,1},{1,0},{2,3},{3,2},{4,5},{5,4},{6,7},{7,6},{8,9},{9,8},{10,11... | collective-permute-start | bytes 9437192 | tf_op jit(solution)/shard_map/ppermute | solution.py:393
  230.6 81.7 %collective-permute-start.25 = (bf16[768,768]{1,0:T(8,128)(2,1)}, bf16[768,768]{1,0:T(8,128)(2,1)}, u32[]{:S(2)}, u32[]{:S(2)}) collective-permute-start(bf16[768,768]{1,0:T(8,128)(2,1)} %constant_dynamic-slice_fusion.1), channel_id=1, source_target_pairs={{0,4},{4,0},{8,12},{12,8},{16,20},{20,16},{24,28},{28,24},{1,5},{5... | collective-permute-start | bytes 3538952 | tf_op jit(solution)/shard_map/ppermute | solution.py:393
  241.9 73.1 %collective-permute-start.18 = (bf16[768,768]{1,0:T(8,128)(2,1)}, bf16[768,768]{1,0:T(8,128)(2,1)}, u32[]{:S(2)}, u32[]{:S(2)}) collective-permute-start(bf16[768,768]{1,0:T(8,128)(2,1)} %constant_dynamic-slice_fusion), channel_id=1, source_target_pairs={{0,4},{4,0},{8,12},{12,8},{16,20},{20,16},{24,28},{28,24},{1,5},{5... | collective-permute-start | bytes 3538952 | tf_op jit(solution)/shard_map/ppermute | solution.py:393
  251.9 65.8 %collective-permute-start.4 = (bf16[512,1536]{1,0:T(8,128)(2,1)}, bf16[512,1536]{1,0:T(8,128)(2,1)}, u32[]{:S(2)}, u32[]{:S(2)}) collective-permute-start(bf16[512,1536]{1,0:T(8,128)(2,1)} %add_convert_fusion.1), channel_id=1, source_target_pairs={{0,2},{1,3},{2,0},{3,1},{4,6},{5,7},{6,4},{7,5},{8,10},{9,11},{10,... | collective-permute-start | bytes 4718600 | tf_op jit(solution)/shard_map/ppermute | solution.py:393
  262.3 38.8 %collective-permute-start.12 = (bf16[92,1536]{1,0:T(8,128)(2,1)S(1)}, bf16[92,1536]{1,0:T(8,128)(2,1)S(1)}, u32[]{:S(2)}, u32[]{:S(2)}) collective-permute-start(bf16[92,1536]{1,0:T(8,128)(2,1)S(1)} %fusion.4), channel_id=1, source_target_pairs={{0,4},{4,0},{8,12},{12,8},{16,20},{20,16},{24,28},{28,24},{1,5},{5... | collective-permute-start | bytes 847880 | tf_op jit(solution)/shard_map/ppermute | solution.py:393
  313.4 21.7 %collective-permute-start.26 = (bf16[384,768]{1,0:T(8,128)(2,1)S(1)}, bf16[384,768]{1,0:T(8,128)(2,1)}, u32[]{:S(2)}, u32[]{:S(2)}) collective-permute-start(bf16[384,768]{1,0:T(8,128)(2,1)S(1)} %add_convert_fusion.2), channel_id=1, source_target_pairs={{0,8},{4,12},{8,0},{12,4},{16,24},{20,28},{24,16},{28,20},{1,9},{5... | collective-permute-start | bytes 1769480 | tf_op jit(solution)/shard_map/ppermute | solution.py:393
  317.2 34.4 %collective-permute-start.19 = (bf16[384,768]{1,0:T(8,128)(2,1)}, bf16[384,768]{1,0:T(8,128)(2,1)}, u32[]{:S(2)}, u32[]{:S(2)}) collective-permute-start(bf16[384,768]{1,0:T(8,128)(2,1)} %add_convert_fusion.3), channel_id=1, source_target_pairs={{0,8},{4,12},{8,0},{12,4},{16,24},{20,28},{24,16},{28,20},{1,9},{5... | collective-permute-start | bytes 1769480 | tf_op jit(solution)/shard_map/ppermute | solution.py:393
  322.5 63.1 %collective-permute-start.5 = (bf16[512,1536]{1,0:T(8,128)(2,1)}, bf16[512,1536]{1,0:T(8,128)(2,1)}, u32[]{:S(2)}, u32[]{:S(2)}) collective-permute-start(bf16[512,1536]{1,0:T(8,128)(2,1)} %quarter.2.value_ref), channel_id=1, source_target_pairs={{0,2},{1,3},{2,0},{3,1},{4,6},{5,7},{6,4},{7,5},{8,10},{9,11},{10,... | collective-permute-start | bytes 4718600 | tf_op jit(solution)/shard_map/ppermute | solution.py:393
  326.8 49.3 %collective-permute-start.16 = (bf16[432,256]{1,0:T(8,128)(2,1)}, bf16[432,256]{1,0:T(8,128)(2,1)}, u32[]{:S(2)}, u32[]{:S(2)}) collective-permute-start(bf16[432,256]{1,0:T(8,128)(2,1)} %reshape.215.refs_0_), channel_id=1, source_target_pairs={{0,2},{1,3},{2,0},{3,1},{4,6},{5,7},{6,4},{7,5},{8,10},{9,11},{10,... | collective-permute-start | bytes 663560 | tf_op jit(solution)/shard_map/ppermute | solution.py:393
  328.3 66.2 %collective-permute-start.15 = (bf16[432,256]{1,0:T(8,128)(2,1)}, bf16[432,256]{1,0:T(8,128)(2,1)}, u32[]{:S(2)}, u32[]{:S(2)}) collective-permute-start(bf16[432,256]{1,0:T(8,128)(2,1)} %reshape.215.refs_0_), channel_id=1, source_target_pairs={{0,1},{1,0},{2,3},{3,2},{4,5},{5,4},{6,7},{7,6},{8,9},{9,8},{10,11... | collective-permute-start | bytes 663560 | tf_op jit(solution)/shard_map/ppermute | solution.py:393
  336.3 18.2 %collective-permute-start.27 = (bf16[192,768]{1,0:T(8,128)(2,1)S(1)}, bf16[192,768]{1,0:T(8,128)(2,1)S(1)}, u32[]{:S(2)}, u32[]{:S(2)}) collective-permute-start(bf16[192,768]{1,0:T(8,128)(2,1)S(1)} %add_convert_fusion.5), channel_id=1, source_target_pairs={{0,16},{4,20},{8,24},{12,28},{16,0},{20,4},{24,8},{28,12},{1,17},{... | collective-permute-start | bytes 884744 | tf_op jit(solution)/shard_map/ppermute | solution.py:393
  352.8 20.0 %collective-permute-start.20 = (bf16[192,768]{1,0:T(8,128)(2,1)S(1)}, bf16[192,768]{1,0:T(8,128)(2,1)S(1)}, u32[]{:S(2)}, u32[]{:S(2)}) collective-permute-start(bf16[192,768]{1,0:T(8,128)(2,1)S(1)} %add_convert_fusion.7), channel_id=1, source_target_pairs={{0,16},{4,20},{8,24},{12,28},{16,0},{20,4},{24,8},{28,12},{1,17},{... | collective-permute-start | bytes 884744 | tf_op jit(solution)/shard_map/ppermute | solution.py:393
  355.7 29.9 %collective-permute-start.28 = (bf16[192,768]{1,0:T(8,128)(2,1)S(1)}, bf16[192,768]{1,0:T(8,128)(2,1)}, u32[]{:S(2)}, u32[]{:S(2)}) collective-permute-start(bf16[192,768]{1,0:T(8,128)(2,1)S(1)} %add_convert_fusion.4.value_ref), channel_id=1, source_target_pairs={{0,16},{4,20},{8,24},{12,28},{16,0},{20,4},{24,8},{28,12},{1,17},{... | collective-permute-start | bytes 884744 | tf_op jit(solution)/shard_map/ppermute | solution.py:393
  374.8 17.0 %collective-permute-start.21 = (bf16[192,768]{1,0:T(8,128)(2,1)}, bf16[192,768]{1,0:T(8,128)(2,1)}, u32[]{:S(2)}, u32[]{:S(2)}) collective-permute-start(bf16[192,768]{1,0:T(8,128)(2,1)} %add_convert_fusion.6.value_ref), channel_id=1, source_target_pairs={{0,16},{4,20},{8,24},{12,28},{16,0},{20,4},{24,8},{28,12},{1,17},{... | collective-permute-start | bytes 884744 | tf_op jit(solution)/shard_map/ppermute | solution.py:393
  376.2 18.3 %collective-permute-start.17 = (bf16[432,256]{1,0:T(8,128)(2,1)}, bf16[432,256]{1,0:T(8,128)(2,1)}, u32[]{:S(2)}, u32[]{:S(2)}) collective-permute-start(bf16[432,256]{1,0:T(8,128)(2,1)} %collective-permute-done.16.refs_2_), channel_id=1, source_target_pairs={{0,1},{1,0},{2,3},{3,2},{4,5},{5,4},{6,7},{7,6},{8,9},{9,8},{10,11... | collective-permute-start | bytes 663560 | tf_op jit(solution)/shard_map/ppermute | solution.py:393
  385.6 67.3 %collective-permute-start.7 = (bf16[512,1536]{1,0:T(8,128)(2,1)}, bf16[512,1536]{1,0:T(8,128)(2,1)S(1)}, u32[]{:S(2)}, u32[]{:S(2)}) collective-permute-start(bf16[512,1536]{1,0:T(8,128)(2,1)} %quarter.2.value_ref), channel_id=1, source_target_pairs={{0,1},{1,0},{2,3},{3,2},{4,5},{5,4},{6,7},{7,6},{8,9},{9,8},{10,11... | collective-permute-start | bytes 4718600 | tf_op jit(solution)/shard_map/ppermute | solution.py:393
  385.6 73.8 %collective-permute-start.6 = (bf16[512,1536]{1,0:T(8,128)(2,1)}, bf16[512,1536]{1,0:T(8,128)(2,1)S(1)}, u32[]{:S(2)}, u32[]{:S(2)}) collective-permute-start(bf16[512,1536]{1,0:T(8,128)(2,1)} %collective-permute-done.5.value_ref), channel_id=1, source_target_pairs={{0,1},{1,0},{2,3},{3,2},{4,5},{5,4},{6,7},{7,6},{8,9},{9,8},{10,11... | collective-permute-start | bytes 4718600 | tf_op jit(solution)/shard_map/ppermute | solution.py:393
  394.5 27.9 %collective-permute-start.22 = (bf16[384,768]{1,0:T(8,128)(2,1)}, bf16[384,768]{1,0:T(8,128)(2,1)}, u32[]{:S(2)}, u32[]{:S(2)}) collective-permute-start(bf16[384,768]{1,0:T(8,128)(2,1)} %join.2.value_ref), channel_id=1, source_target_pairs={{0,8},{4,12},{8,0},{12,4},{16,24},{20,28},{24,16},{28,20},{1,9},{5... | collective-permute-start | bytes 1769480 | tf_op jit(solution)/shard_map/ppermute | solution.py:393
  407.4 34.3 %collective-permute-start.24 = (bf16[384,768]{1,0:T(8,128)(2,1)}, bf16[384,768]{1,0:T(8,128)(2,1)}, u32[]{:S(2)}, u32[]{:S(2)}) collective-permute-start(bf16[384,768]{1,0:T(8,128)(2,1)} %join.2.value_ref), channel_id=1, source_target_pairs={{0,4},{4,0},{8,12},{12,8},{16,20},{20,16},{24,28},{28,24},{1,5},{5... | collective-permute-start | bytes 1769480 | tf_op jit(solution)/shard_map/ppermute | solution.py:393
  411.0 34.9 %collective-permute-start.30 = (bf16[384,768]{1,0:T(8,128)(2,1)}, bf16[384,768]{1,0:T(8,128)(2,1)}, u32[]{:S(2)}, u32[]{:S(2)}) collective-permute-start(bf16[384,768]{1,0:T(8,128)(2,1)} %collective-permute-done.29.value_ref), channel_id=1, source_target_pairs={{0,4},{4,0},{8,12},{12,8},{16,20},{20,16},{24,28},{28,24},{1,5},{5... | collective-permute-start | bytes 1769480 | tf_op jit(solution)/shard_map/ppermute | solution.py:393
  422.4 25.7 %collective-permute-start.23 = (bf16[384,768]{1,0:T(8,128)(2,1)}, bf16[384,768]{1,0:T(8,128)(2,1)}, u32[]{:S(2)}, u32[]{:S(2)}) collective-permute-start(bf16[384,768]{1,0:T(8,128)(2,1)} %collective-permute-done.22.value_ref), channel_id=1, source_target_pairs={{0,4},{4,0},{8,12},{12,8},{16,20},{20,16},{24,28},{28,24},{1,5},{5... | collective-permute-start | bytes 1769480 | tf_op jit(solution)/shard_map/ppermute | solution.py:393
  (27 other events, 293.5 us)
Sparse Core Ops, SparseCore 0:
  168.9 115.3 all-reduce.8
Sparse Core Ops, SparseCore 1:
  215.7 56.9 all-gather.1
